TPU v7x, 128 devices: a whole 4x4x4 slice. The times are simulated.
128 devices in a mesh: row: 8 (over y, core), col: 16 (over z, x).
Axes of the slice: x: 4, y: 4, z: 4, core: 2. Of those that a mesh axis runs over, the one named last changes fastest.
Arguments:
- kernel_panel: float32 [64, 32768], P(None, ('row', 'col')), may hold values from -4 to 16, as said below
- kernel_slab: float32 [32768, 4096], P('row', 'col'), may hold values from -4 to 20, as said below
- targets: float32 [256, 32768], P(None, ('row', 'col')), may hold values from -6 to 6
Outputs:
- updated_slab: float32 [32768, 4096], P('row', 'col')
- solved_targets: float32 [256, 32768], P('col', 'row')
- panel_factor: float32 [64, 32768], P(None, ('row', 'col'))
Inputs may be any that keep to these rules, and one draw needn't show every extreme that they name: kernel_panel[:, 0:64] is symmetric and positive definite. `kernel_slab`: rows 0 to 63 equal kernel_panel[:, 32768 - 4096 : 32768]; the last 4096 rows form a symmetric matrix.
All inputs are finite; a program needn't handle non-finite values.
Results may differ from a plain program's by a relative error of at most 0.00018.
Values sent between devices are 32-bit elements; how exact they have to be, the bound alone decides.
No kernel may reach another device: no remote copies, remote signals or barrier semaphores. Data moves between devices by JAX's collectives and lax.ppermute only.
A program may use at most 64 MiB of HBM per device.

v0:
```python
import jax
import jax.numpy as jnp
from jax import lax
from jax.sharding import PartitionSpec as P


def spread(block, axis, source):
    block = jnp.where(lax.axis_index(axis) == source, block, jnp.zeros_like(block))
    return lax.psum(block, axis)


def lower_solve(factor, values):
    return jax.scipy.linalg.solve_triangular(factor, values, lower=True)


def body(kernel_panel, kernel_slab, targets):
    highest = lax.Precision.HIGHEST
    panel_width = kernel_panel.shape[0]
    row_count = lax.axis_size("row")
    row_index = lax.axis_index("row")
    flat_index = lax.axis_index(("row", "col"))
    corner_rows = jnp.concatenate([kernel_panel[:, :panel_width], targets[:, :panel_width]], 0)
    shared = spread(corner_rows, ("row", "col"), 0)
    lower_factor = jnp.linalg.cholesky(shared[:panel_width])
    panel_factor = lower_solve(lower_factor, kernel_panel)
    gathered = lax.all_gather(panel_factor, "col", axis=1, tiled=True)
    slab_factor = spread(panel_factor, "row", row_count - 1)
    product = lax.dot_general(
        gathered,
        slab_factor,
        (((0,), (0,)), ((), ())),
        precision=highest,
        preferred_element_type=jnp.float32,
    )
    update = kernel_slab - product
    head_rows = jnp.where(row_index == 0, slab_factor, update[:panel_width])
    updated_slab = jnp.concatenate([head_rows, update[panel_width:]], 0)
    solved_lead = lower_solve(lower_factor, shared[panel_width:].T).T
    result = targets - jnp.dot(
        solved_lead, panel_factor, precision=highest, preferred_element_type=jnp.float32
    )
    head_cols = jnp.where(flat_index == 0, solved_lead, result[:, :panel_width])
    result = jnp.concatenate([head_cols, result[:, panel_width:]], 1)
    solved_targets = lax.all_to_all(result, "col", split_axis=0, concat_axis=1, tiled=True)
    return (updated_slab, solved_targets, panel_factor)


def solution(mesh):
    in_specs = (P(None, ("row", "col")), P("row", "col"), P(None, ("row", "col")))
    out_specs = (P("row", "col"), P("col", "row"), P(None, ("row", "col")))
    return jax.shard_map(body, mesh=mesh, in_specs=in_specs, out_specs=out_specs, check_vma=False)
```

profile of v0, /device:TPU:24, one launch (start us, length us, event | category | flops | bytes accessed | tf_op | source)
XLA Modules:
  0.0 286.4 jit_solution(15664791899250229156)
XLA Ops:
  7.2 0.0 all-reduce.3.cloned.1.call-start
  7.2 0.8 slice.34
  8.0 0.1 copy.22
  8.1 1.1 copy.17
  9.2 0.7 maximum_select_fusion
  9.9 0.0 all-reduce.3.cloned.1.call-update
  9.9 0.0 all-reduce.5.cloned.1.call-start
  10.0 142.1 %all-reduce.3.cloned.1.call-done = f32[320,64]{0,1:T(8,128)} async-done(((f32[320,64]{0,1:T(8,128)}), f32[320,64]{0,1:T(8,128)}) %all-reduce.3.cloned.1.call-update) | async-done | bytes 81936 | tf_op jit(solution)/shard_map/psum | solution.py:9
  152.1 0.8 slice.43
  152.9 0.1 copy.18
  152.9 0.8 fusion.5
  153.7 5.8 %cholesky.18 = f32[64,64]{1,0:T(8,128)S(1)} custom-call(f32[64,64]{1,0:T(8,128)S(1)} %fusion.5), custom_call_target="Cholesky" | custom-call | tf_op jit(solution)/shard_map/jit(cholesky)/cholesky | solution.py:24
  159.6 0.6 compare_reduce_fusion
  160.2 0.7 fusion.1
  160.9 4.9 %custom-call.7 = f32[1,64,64]{1,2,0:T(8,128)S(1)} custom-call(f32[1,64,64]{2,1,0:T(8,128)S(1)} %fusion.1), custom_call_target="InvertDiagBlocksLowerTriangular" | custom-call | tf_op jit(solution)/shard_map/jit(_solve_triangular)/triangular_solve | solution.py:13
  165.8 1.8 broadcast_select_fusion
  167.5 0.0 all-reduce.5.cloned.1.call-update
  167.6 0.0 all-gather.2.cloned.1.call-start
  167.6 0.7 all-gather.2.cloned.1.call-update
  168.3 1.2 fusion
  169.5 1.3 convolution_subtract_fusion.1
  170.8 0.8 copy.20
  171.7 4.6 %all-to-all-start = ((f32[16,16,256]{2,1,0:T(8,128)}), f32[16,16,256]{2,1,0:T(8,128)S(1)}, u32[]{:S(2)}, u32[]{:S(2)}) async-start(f32[16,16,256]{2,1,0:T(8,128)} %bitcast.7), calls=%async_computation | async-start | bytes 524288 | tf_op jit(solution)/shard_map/all_to_all | solution.py:44
  176.3 8.9 %all-to-all-done = f32[16,16,256]{2,1,0:T(8,128)S(1)} async-done(((f32[16,16,256]{2,1,0:T(8,128)}), f32[16,16,256]{2,1,0:T(8,128)S(1)}, u32[]{:S(2)}, u32[]{:S(2)}) %all-to-all-start) | async-done | bytes 262176 | tf_op jit(solution)/shard_map/all_to_all | solution.py:44
  185.2 0.7 copy.23
  185.9 37.4 %all-reduce.5.cloned.1.call-done = f32[64,256]{1,0:T(8,128)} async-done(((f32[64,256]{1,0:T(8,128)}), f32[64,256]{1,0:T(8,128)}) %all-reduce.5.cloned.1.call-update) | async-done | bytes 65552 | tf_op jit(solution)/shard_map/psum | solution.py:9
  223.3 47.4 %all-gather.2.cloned.1.call-done = f32[64,4096]{1,0:T(8,128)} async-done(((f32[64,256]{1,0:T(8,128)}), f32[64,4096]{1,0:T(8,128)}) %all-gather.2.cloned.1.call-update) | async-done | bytes 1048592 | tf_op jit(solution)/shard_map/all_gather | solution.py:26
  270.7 6.0 %convolution_subtract_fusion = f32[4096,256]{1,0:T(8,128)S(1)} fusion(f32[4096,256]{1,0:T(8,128)} %param.6, f32[64,4096]{1,0:T(8,128)} %all-gather.2.cloned.1.call-done, f32[64,256]{1,0:T(8,128)} %all-reduce.5.cloned.1.call-done), kind=kOutput, calls=%fused_computation | convolution fusion | flops 806354944 | bytes 9502720 | tf_op jit(solution)/shard_map/dot_general | solution.py:28
  276.7 0.0 copy-start
  276.8 0.3 slice.45
  277.0 0.6 copy-done
  277.6 2.3 pad_maximum_fusion
  (6 shorter events, 0.1 us)
Async XLA Ops:
  7.2 144.9 %all-reduce.3.cloned.1.call-start = ((), (), s32[]{:S(2)}) async-start(), calls=%async_computation.1 | async-start | bytes 196608 | tf_op jit(solution)/shard_map/psum | solution.py:9
  9.9 213.4 %all-reduce.5.cloned.1.call-start = ((), (), s32[]{:S(2)}) async-start(), calls=%async_computation.2 | async-start | bytes 131072 | tf_op jit(solution)/shard_map/psum | solution.py:9
  167.6 103.2 %all-gather.2.cloned.1.call-start = ((), (), s32[]{:S(2)}) async-start(), calls=%async_computation.3 | async-start | bytes 1114112 | tf_op jit(solution)/shard_map/all_gather | solution.py:26
  171.7 13.6 %all-to-all-start = ((f32[16,16,256]{2,1,0:T(8,128)}), f32[16,16,256]{2,1,0:T(8,128)S(1)}, u32[]{:S(2)}, u32[]{:S(2)}) async-start(f32[16,16,256]{2,1,0:T(8,128)} %bitcast.7), calls=%async_computation | async-start | bytes 524288 | tf_op jit(solution)/shard_map/all_to_all | solution.py:44
  276.7 0.8 copy-start
Sparse Core Ops, SparseCore 0:
  13.3 138.7 all-reduce.2
  167.7 55.5 all-reduce.4
  226.0 44.6 all-gather.1
where the time goes:
time: 287 us; the launch traced here: 286 us
  waiting for transfers between devices  237 us (83%)
  other arithmetic  15.9 us (6%)
  between operations  13.9 us (5%)
  matrix products  10.2 us (4%)
  local copies, waits for them, and re-layouts  5.16 us (2%)
  starting transfers between devices  4.74 us (2%)
    psum x2, waiting for transfers between devices, spread(): return lax.psum(block, axis)  179 us
    all_gather x1, waiting for transfers between devices, body(): gathered = lax.all_gather(panel_factor, 'col', axis=1, tiled=True)  47.4 us
    all_to_all x1, waiting for transfers between devices, body(): lax.all_to_all(result, 'col', split_axis=0, concat_axis=1, tiled=True)  8.92 us
    another operation x3, other arithmetic, body(): lower_factor = jnp.linalg.cholesky(shared[:panel_width])  6.52 us
    dot_general x1, matrix products, body(): lax.dot_general(gathered, slab_factor, (((0,), (0,)), ((), ())), precisio...  6 us
  transfers between devices with their start and end apart: 4, of which 4 were waited for; matrix products, arithmetic and copies ran while one was open for 1% of the time, Pallas kernels for 0%

commit v1 on v0

v1 whole, which is shorter than its diff:
```python
import jax
import jax.numpy as jnp
from jax import lax
from jax.sharding import PartitionSpec as P

HIGHEST = lax.Precision.HIGHEST


def lower_solve(factor, values):
    return jax.scipy.linalg.solve_triangular(factor, values, lower=True)


def from_first(value, axis):
    size, index = lax.axis_size(axis), lax.axis_index(axis)
    reach = size
    while reach > 1:
        half = reach // 2
        pairs = [(i, i + half) for i in range(0, size, reach)]
        arrived = lax.ppermute(value, axis, pairs)
        value = jnp.where(index % reach == half, arrived, value)
        reach = half
    return value


def body(kernel_panel, kernel_slab, targets):
    width = kernel_panel.shape[0]
    cols = lax.axis_size("col")
    row_index = lax.axis_index("row")
    col_index = lax.axis_index("col")
    wide = kernel_panel.shape[1]
    mine = targets.shape[0] // cols
    pieces = jnp.broadcast_to(kernel_panel[None], (cols,) + kernel_panel.shape)
    sent = jnp.concatenate([pieces, targets.reshape(cols, mine, wide)], 1)
    got = lax.all_to_all(sent, "col", split_axis=0, concat_axis=0)
    lead = jnp.concatenate([kernel_panel[:, :width], targets[:, :width].T], 1)
    down = from_first(jnp.concatenate([kernel_slab[:width], lead], 1), "row")
    slab_panel, lead = down[:, :wide], down[:, wide:]
    corner = jnp.broadcast_to(lead[:, :width][None], (cols, width, width))
    heads = lead[:, width:].reshape(width, cols, mine).transpose(1, 0, 2)
    small = lax.all_to_all(jnp.concatenate([corner, heads], 2), "col", split_axis=0, concat_axis=0)[0]
    lower_factor = jnp.linalg.cholesky(small[:, :width])
    raw = got[:, :width].transpose(1, 0, 2).reshape(width, cols * wide)
    solved = lower_solve(lower_factor, jnp.concatenate([raw, slab_panel, kernel_panel, small[:, width:]], 1))
    gathered = solved[:, : cols * wide]
    slab_factor = solved[:, cols * wide : cols * wide + wide]
    panel_factor = solved[:, cols * wide + wide : cols * wide + 2 * wide]
    solved_lead = solved[:, cols * wide + 2 * wide :].T
    product = lax.dot_general(
        gathered, slab_factor, (((0,), (0,)), ((), ())), precision=HIGHEST, preferred_element_type=jnp.float32
    )
    update = kernel_slab - product
    head_rows = jnp.where(row_index == 0, slab_factor, update[:width])
    updated_slab = jnp.concatenate([head_rows, update[width:]], 0)
    rows = got[:, width:].transpose(1, 0, 2).reshape(mine, cols * wide)
    result = rows - jnp.dot(solved_lead, gathered, precision=HIGHEST, preferred_element_type=jnp.float32)
    head_cols = jnp.where(row_index == 0, solved_lead, result[:, :width])
    solved_targets = jnp.concatenate([head_cols, result[:, width:]], 1)
    return (updated_slab, solved_targets, panel_factor)


def solution(mesh):
    in_specs = (P(None, ("row", "col")), P("row", "col"), P(None, ("row", "col")))
    out_specs = (P("row", "col"), P("col", "row"), P(None, ("row", "col")))
    return jax.shard_map(body, mesh=mesh, in_specs=in_specs, out_specs=out_specs, check_vma=False)
```

time: 287 us -> 90.6 us (0.32)
  waiting for transfers between devices: 237 us -> 33.1 us
  between operations: 13.9 us -> 0.95 us
  starting transfers between devices: 4.74 us -> 15 us
  other arithmetic: 15.9 us -> 21 us
  local copies, waits for them, and re-layouts: 5.16 us -> 9.25 us
    psum x2 -> x0, waiting for transfers between devices: 179 us -> none  [spread(): return lax.psum(block, axis)]
    all_gather x1 -> x0, waiting for transfers between devices: 47.4 us -> none  [body(): gathered = lax.all_gather(panel_factor, 'col', axis=1, tiled=True)]
    ppermute x0 -> x3, waiting for transfers between devices: none -> 16 us  [from_first(): arrived = lax.ppermute(value, axis, pairs)]
    all_to_all x1 -> x2, waiting for transfers between devices: 8.92 us -> 17.1 us  [the longest x1 10.8 us: body(): lax.all_to_all(jnp.concatenate([corner, heads], 2), 'col', split_axis=0,...]
    all_to_all x1 -> x2, starting transfers between devices: 4.62 us -> 11.7 us  [the longest x1 8.02 us: body(): lax.all_to_all(jnp.concatenate([corner, heads], 2), 'col', split_axis=0,...]
    concatenate x2 -> x5, other arithmetic: 2.3 us -> 7.5 us  [the longest x1 4.45 us: body(): updated_slab = jnp.concatenate([head_rows, update[width:]], 0)]
    slice x6 -> x15, local copies, waits for them, and re-layouts: 1.89 us -> 5.55 us  [the longest x1 2.18 us: body(): updated_slab = jnp.concatenate([head_rows, update[width:]], 0)]
    ppermute x0 -> x3, starting transfers between devices: none -> 3.28 us  [from_first(): arrived = lax.ppermute(value, axis, pairs)]
  transfers between devices with their start and end apart: 4 -> 5, of which waited for: 4 -> 4; matrix products, arithmetic and copies ran while one was open for 1% -> 17% of each run, Pallas kernels for 0% -> 0%
where the time goes in v1:
time: 90.6 us; the launch traced here: 90 us
  waiting for transfers between devices  33.1 us (37%)
  other arithmetic  21 us (23%)
  starting transfers between devices  15 us (17%)
  matrix products  10.8 us (12%)
  local copies, waits for them, and re-layouts  9.25 us (10%)
  between operations  0.95 us (1%)
    ppermute x3, waiting for transfers between devices, from_first(): arrived = lax.ppermute(value, axis, pairs)  16 us
    all_to_all x1, waiting for transfers between devices, body(): lax.all_to_all(jnp.concatenate([corner, heads], 2), 'col', split_axis=0,...  10.8 us
    all_to_all x1, starting transfers between devices, body(): lax.all_to_all(jnp.concatenate([corner, heads], 2), 'col', split_axis=0,...  8.02 us
    another operation x3, other arithmetic, body(): lower_factor = jnp.linalg.cholesky(small[:, :width])  6.52 us
    all_to_all x1, waiting for transfers between devices, body(): got = lax.all_to_all(sent, 'col', split_axis=0, concat_axis=0)  6.3 us
    another operation x2, other arithmetic, lower_solve(): return jax.scipy.linalg.solve_triangular(factor, values, lower=True)  6.18 us
    dot_general x1, matrix products, body(): lax.dot_general(gathered, slab_factor, (((0,), (0,)), ((), ())), precisio...  5.34 us
    concatenate x1, other arithmetic, body(): updated_slab = jnp.concatenate([head_rows, update[width:]], 0)  4.45 us
  transfers between devices with their start and end apart: 5, of which 4 were waited for; matrix products, arithmetic and copies ran while one was open for 17% of the time, Pallas kernels for 0%

profile of v1, /device:TPU:24, one launch (start us, length us, event | category | flops | bytes accessed | tf_op | source)
XLA Modules:
  0.0 90.0 jit_solution(13936352368751797273)
XLA Ops:
  0.6 0.8 slice.73
  1.4 0.1 copy.40
  1.5 0.9 slice.72
  2.3 0.1 copy.39
  2.4 0.9 %slice_bitcast_fusion.2 = f32[64,256]{0,1:T(8,128)S(1)} fusion(f32[256,256]{1,0:T(8,128)} %param.5), kind=kLoop, calls=%fused_computation.22 | loop fusion | bytes 131072 | tf_op jit(solution)/shard_map/transpose | solution.py:35
  3.4 0.7 collective-permute-start
  4.1 0.0 collective-permute-done
  4.1 1.3 %collective-permute-start.1 = (f32[64,576]{0,1:T(8,128)S(1)}, f32[64,576]{0,1:T(8,128)S(1)}, u32[]{:S(2)}, u32[]{:S(2)}) collective-permute-start(f32[64,576]{0,1:T(8,128)S(1)} %broadcast_select_fusion), channel_id=1, source_target_pairs={{0,32},{64,96},{1,33},{65,97},{2,34},{66,98},{3,35},{67,99},{4,36}... | collective-permute-start | bytes 442376 | tf_op jit(solution)/shard_map/ppermute | solution.py:19
  5.4 14.8 %collective-permute-done.1 = f32[64,576]{0,1:T(8,128)S(1)} collective-permute-done((f32[64,576]{0,1:T(8,128)S(1)}, f32[64,576]{0,1:T(8,128)S(1)}, u32[]{:S(2)}, u32[]{:S(2)}) %collective-permute-start.1) | collective-permute-done | bytes 147488 | tf_op jit(solution)/shard_map/ppermute | solution.py:19
  20.3 1.3 %collective-permute-start.2 = (f32[64,576]{0,1:T(8,128)S(1)}, f32[64,576]{0,1:T(8,128)S(1)}, u32[]{:S(2)}, u32[]{:S(2)}) collective-permute-start(f32[64,576]{0,1:T(8,128)S(1)} %broadcast_select_fusion.1), channel_id=1, source_target_pairs={{0,16},{32,48},{64,80},{96,112},{1,17},{33,49},{65,81},{97,113},{2... | collective-permute-start | bytes 442376 | tf_op jit(solution)/shard_map/ppermute | solution.py:19
  21.6 1.2 %collective-permute-done.2 = f32[64,576]{0,1:T(8,128)S(1)} collective-permute-done((f32[64,576]{0,1:T(8,128)S(1)}, f32[64,576]{0,1:T(8,128)S(1)}, u32[]{:S(2)}, u32[]{:S(2)}) %collective-permute-start.2) | collective-permute-done | bytes 147488 | tf_op jit(solution)/shard_map/ppermute | solution.py:19
  22.9 0.1 copy.27
  22.9 0.2 copy.28
  23.2 0.0 copy-start.2
  23.2 1.0 %pad_maximum_fusion.2 = f32[16,64,80]{2,1,0:T(8,128)} fusion(f32[16,64,16]{2,1,0:T(8,128)S(1)} %copy.28, f32[16,64,64]{2,1,0:T(8,128)S(1)} %broadcast_in_dim.5), kind=kLoop, calls=%fused_computation.15 | loop fusion | flops 81920 | bytes 655360 | tf_op jit(solution)/shard_map/concatenate | solution.py:40
  24.2 0.0 copy-start.1
  24.2 8.0 %all-to-all-start = ((f32[16,64,80]{2,1,0:T(8,128)}), f32[16,64,80]{2,1,0:T(8,128)S(1)}, u32[]{:S(2)}, u32[]{:S(2)}) async-start(f32[16,64,80]{2,1,0:T(8,128)} %pad_maximum_fusion.2), calls=%async_computation | async-start | bytes 1048576 | tf_op jit(solution)/shard_map/all_to_all | solution.py:40
  32.3 0.0 copy-done.2
  32.3 0.1 broadcast_in_dim.6
  32.4 0.0 copy-done.1
  32.4 1.2 %pad_maximum_fusion.1 = f32[16,80,256]{2,1,0:T(8,128)} fusion(f32[16,16,256]{2,1,0:T(8,128)S(1)} %bitcast.27, f32[16,64,256]{2,1,0:T(8,128)S(1)} %broadcast_in_dim.6), kind=kLoop, calls=%fused_computation.3 | loop fusion | flops 327680 | bytes 2621440 | tf_op jit(solution)/shard_map/concatenate | solution.py:33
  33.5 10.8 %all-to-all-done = f32[16,64,80]{2,1,0:T(8,128)S(1)} async-done(((f32[16,64,80]{2,1,0:T(8,128)}), f32[16,64,80]{2,1,0:T(8,128)S(1)}, u32[]{:S(2)}, u32[]{:S(2)}) %all-to-all-start) | async-done | bytes 327712 | tf_op jit(solution)/shard_map/all_to_all | solution.py:40
  44.3 3.7 %all-to-all-start.1 = ((f32[16,80,256]{2,1,0:T(8,128)}), f32[16,80,256]{2,1,0:T(8,128)S(1)}, u32[]{:S(2)}, u32[]{:S(2)}) async-start(f32[16,80,256]{2,1,0:T(8,128)} %pad_maximum_fusion.1), calls=%async_computation.1 | async-start | bytes 2621440 | tf_op jit(solution)/shard_map/all_to_all | solution.py:34
  48.0 0.1 copy.32
  48.1 0.1 copy.41
  48.2 0.7 copy.33
  48.9 0.1 copy.30
  49.0 5.8 %cholesky.16 = f32[64,64]{1,0:T(8,128)S(1)} custom-call(f32[64,64]{1,0:T(8,128)S(1)} %fusion.13), custom_call_target="Cholesky" | custom-call | tf_op jit(solution)/shard_map/jit(cholesky)/cholesky | solution.py:41
  54.9 0.6 compare_reduce_fusion
  55.6 0.7 fusion.11
  56.2 5.5 %custom-call.7 = f32[1,64,64]{1,2,0:T(8,128)} custom-call(f32[1,64,64]{2,1,0:T(8,128)S(1)} %fusion.11), custom_call_target="InvertDiagBlocksLowerTriangular" | custom-call | tf_op jit(solution)/shard_map/jit(_solve_triangular)/triangular_solve | solution.py:10
  61.7 6.3 %all-to-all-done.1 = f32[16,80,256]{2,1,0:T(8,128)S(1)} async-done(((f32[16,80,256]{2,1,0:T(8,128)}), f32[16,80,256]{2,1,0:T(8,128)S(1)}, u32[]{:S(2)}, u32[]{:S(2)}) %all-to-all-start.1) | async-done | bytes 1310752 | tf_op jit(solution)/shard_map/all_to_all | solution.py:34
  68.1 0.1 slice_bitcast_fusion
  68.1 0.1 copy.42
  68.3 0.6 copy.34
  68.9 1.9 %fusion = f32[64,4624]{1,0:T(8,128)S(1)} fusion(f32[64,16]{1,0:T(8,128)} %copy.33, f32[64,256]{1,0:T(8,128)S(1)} %copy-done.2, f32[64,256]{1,0:T(8,128)S(1)} %copy.32, f32[64,4096]{1,0:T(8,128)S(1)} %bitcast.26, f32[1,64,64]{1,2,0:T(8,128)} %custom-call.7), kind=kOutput, calls=%fused_computation.4 | convolution fusion | flops 228166656 | bytes 2383872 | tf_op jit(solution)/shard_map/jit(_solve_triangular)/triangular_solve | solution.py:10
  70.8 5.3 %convolution_subtract_fusion = f32[4096,256]{1,0:T(8,128)S(1)} fusion(f32[4096,256]{1,0:T(8,128)} %param.4, f32[64,4624]{1,0:T(8,128)S(1)} %fusion), kind=kOutput, calls=%fused_computation | convolution fusion | flops 806354944 | bytes 9502720 | tf_op jit(solution)/shard_map/dot_general | solution.py:48
  76.2 3.5 %convolution_subtract_fusion.1 = f32[16,4096]{0,1:T(8,128)S(1)} fusion(f32[16,4096]{0,1:T(8,128)S(1)} %bitcast.25, f32[64,4624]{1,0:T(8,128)S(1)} %fusion), kind=kOutput, calls=%fused_computation.1 | convolution fusion | flops 50397184 | bytes 3440640 | tf_op jit(solution)/shard_map/dot_general | solution.py:55
  79.7 0.0 copy-start
  79.7 1.3 %copy-done = f32[16,4096]{0,1:T(8,128)} copy-done((f32[16,4096]{0,1:T(8,128)}, f32[16,4096]{0,1:T(8,128)S(1)}, u32[]{:S(2)}) %copy-start) | copy-done | bytes 262168
  81.0 0.6 fusion.16
  81.6 0.0 slice-start
  81.6 2.2 %slice.101 = f32[4032,256]{1,0:T(8,128)} slice(f32[4096,256]{1,0:T(8,128)S(1)} %convolution_subtract_fusion), slice={[64:4096], [0:256]} | slice | bytes 8257536 | tf_op jit(solution)/shard_map/slice | solution.py:53
  83.8 0.2 slice-done
  84.0 0.6 copy.37
  84.6 0.1 copy.36
  84.7 0.9 pad_maximum_fusion.4
  85.5 4.5 %pad_maximum_fusion = f32[4096,256]{1,0:T(8,128)} fusion(f32[4032,256]{1,0:T(8,128)} %slice.101, f32[64,256]{1,0:T(8,128)S(1)} %get-tuple-element.7), kind=kLoop, calls=%fused_computation.2 | loop fusion | flops 1048576 | bytes 8388608 | tf_op jit(solution)/shard_map/concatenate | solution.py:53
  (14 shorter events, 0.3 us)
Async XLA Ops:
  3.4 0.7 collective-permute-start
  4.1 16.1 %collective-permute-start.1 = (f32[64,576]{0,1:T(8,128)S(1)}, f32[64,576]{0,1:T(8,128)S(1)}, u32[]{:S(2)}, u32[]{:S(2)}) collective-permute-start(f32[64,576]{0,1:T(8,128)S(1)} %broadcast_select_fusion), channel_id=1, source_target_pairs={{0,32},{64,96},{1,33},{65,97},{2,34},{66,98},{3,35},{67,99},{4,36}... | collective-permute-start | bytes 442376 | tf_op jit(solution)/shard_map/ppermute | solution.py:19
  20.3 2.5 %collective-permute-start.2 = (f32[64,576]{0,1:T(8,128)S(1)}, f32[64,576]{0,1:T(8,128)S(1)}, u32[]{:S(2)}, u32[]{:S(2)}) collective-permute-start(f32[64,576]{0,1:T(8,128)S(1)} %broadcast_select_fusion.1), channel_id=1, source_target_pairs={{0,16},{32,48},{64,80},{96,112},{1,17},{33,49},{65,81},{97,113},{2... | collective-permute-start | bytes 442376 | tf_op jit(solution)/shard_map/ppermute | solution.py:19
  23.2 9.1 %copy-start.2 = (f32[64,256]{1,0:T(8,128)S(1)}, f32[64,256]{1,0:T(8,128)}, u32[]{:S(2)}) copy-start(f32[64,256]{1,0:T(8,128)} %param.3) | copy-start | bytes 196612
  24.2 8.1 %copy-start.1 = (f32[256,256]{1,0:T(8,128)S(1)}, f32[256,256]{1,0:T(8,128)}, u32[]{:S(2)}) copy-start(f32[256,256]{1,0:T(8,128)} %param.5) | copy-start | bytes 786436
  24.2 20.1 %all-to-all-start = ((f32[16,64,80]{2,1,0:T(8,128)}), f32[16,64,80]{2,1,0:T(8,128)S(1)}, u32[]{:S(2)}, u32[]{:S(2)}) async-start(f32[16,64,80]{2,1,0:T(8,128)} %pad_maximum_fusion.2), calls=%async_computation | async-start | bytes 1048576 | tf_op jit(solution)/shard_map/all_to_all | solution.py:40
  44.3 23.7 %all-to-all-start.1 = ((f32[16,80,256]{2,1,0:T(8,128)}), f32[16,80,256]{2,1,0:T(8,128)S(1)}, u32[]{:S(2)}, u32[]{:S(2)}) async-start(f32[16,80,256]{2,1,0:T(8,128)} %pad_maximum_fusion.1), calls=%async_computation.1 | async-start | bytes 2621440 | tf_op jit(solution)/shard_map/all_to_all | solution.py:34
  79.7 1.3 %copy-start = (f32[16,4096]{0,1:T(8,128)}, f32[16,4096]{0,1:T(8,128)S(1)}, u32[]{:S(2)}) copy-start(f32[16,4096]{0,1:T(8,128)S(1)} %convolution_subtract_fusion.1) | copy-start | bytes 786436
  81.6 2.4 %slice-start = ((f32[16,4096]{0,1:T(8,128)}), f32[16,4032]{0,1:T(8,128)S(1)}, s32[]{:S(2)}) async-start(f32[16,4096]{0,1:T(8,128)} %copy-done), calls=%async_computation.2 | async-start | bytes 4128768 | tf_op jit(solution)/shard_map/slice | solution.py:57

commit v2 on v1

v2 whole, which is shorter than its diff:
```python
import jax
import jax.numpy as jnp
from jax import lax
from jax.experimental import pallas as pl
from jax.experimental.pallas import tpu as pltpu
from jax.sharding import PartitionSpec as P

HIGHEST = lax.Precision.HIGHEST
LANES = 128
SUB = 8


def invert_kernel(lead_ref, inverse_ref):
    width = inverse_ref.shape[0]
    count = width // SUB
    lane = lax.broadcasted_iota(jnp.int32, (SUB, LANES), 1)
    row = lax.broadcasted_iota(jnp.int32, (SUB, LANES), 0)
    blocks = []
    for i in range(count):
        unit = jnp.where(lane - width == row + i * SUB, 1.0, 0.0).astype(jnp.float32)
        blocks.append(jnp.where(lane < width, lead_ref[i * SUB : (i + 1) * SUB, :], unit))
    shape = (SUB, LANES)
    for b in range(count):
        below = range(b + 1, count)
        spread = [
            {i: jnp.broadcast_to(blocks[i][:, b * SUB + j : b * SUB + j + 1], shape) for i in range(b, count)}
            for j in range(SUB)
        ]
        for j in range(SUB):
            pivot = jnp.broadcast_to(spread[j][b][j : j + 1, :], shape)
            scale = lax.rsqrt(pivot)
            scale = scale * (1.5 - 0.5 * (pivot * scale) * scale)
            top = jnp.broadcast_to(blocks[b][j : j + 1, :], shape) * scale
            factor = {i: spread[j][i] * scale for i in below}
            factor[b] = jnp.where(row > j, spread[j][b] * scale, 0.0)
            for k in range(j + 1, SUB):
                entry = jnp.broadcast_to(spread[k][b][j : j + 1, :], shape) * scale
                for i in range(b, count):
                    spread[k][i] = spread[k][i] - factor[i] * entry
            blocks[b] = jnp.where(row == j, top, blocks[b] - factor[b] * top)
            for i in below:
                blocks[i] = blocks[i] - factor[i] * top
    for i in range(count):
        inverse_ref[i * SUB : (i + 1) * SUB, :] = blocks[i][:, width:]


def invert(lead, width):
    return pl.pallas_call(
        invert_kernel,
        out_shape=jax.ShapeDtypeStruct((width, width), jnp.float32),
        in_specs=[pl.BlockSpec(memory_space=pltpu.VMEM)],
        out_specs=pl.BlockSpec(memory_space=pltpu.VMEM),
        cost_estimate=pl.CostEstimate(flops=4 * width**3, bytes_accessed=8 * width**2, transcendentals=width),
        name="invert_factor",
    )(lead)


def halves(value):
    high = value.astype(jnp.bfloat16)
    return high, (value - high.astype(jnp.float32)).astype(jnp.bfloat16)


def update_kernel(first_ref, one_ref, two_ref, inverse_ref, down_ref, panel_ref, slab_ref,
                  slab_out, targets_out, factor_out, held, arrive, leave):
    count, depth = one_ref.shape[0], one_ref.shape[1]
    width = inverse_ref.shape[0]
    wide = panel_ref.shape[1]
    pieces = [pl.ds(p * wide, wide) for p in range(count)]
    loads = [pltpu.make_async_copy(slab_ref.at[piece], held.at[piece], arrive.at[p]) for p, piece in enumerate(pieces)]
    stores = [pltpu.make_async_copy(held.at[piece], slab_out.at[piece], leave.at[p]) for p, piece in enumerate(pieces)]
    for load in loads:
        load.start()
    inverse = inverse_ref[...]

    def solve(values):
        return jnp.dot(inverse, values, precision=HIGHEST, preferred_element_type=jnp.float32)

    factor_out[...] = solve(panel_ref[...])
    slab_panel = jnp.concatenate([down_ref[depth : depth + width, :], down_ref[depth + width :, :]], 1)
    slab_factor = solve(slab_panel)
    slab_high, slab_low = halves(slab_factor)
    slab_stack = jnp.concatenate([slab_high, slab_low, slab_high], 0)
    lead = lax.dot_general(
        down_ref[width:depth, :width], inverse, (((1,), (1,)), ((), ())),
        precision=HIGHEST, preferred_element_type=jnp.float32,
    )
    is_first = first_ref[0] == 1
    for p in range(count):
        raw = jnp.concatenate([one_ref[p, :width, :], two_ref[p, :width, :]], 1)
        solved = solve(raw)
        high, low = halves(solved)
        stack = jnp.concatenate([high, high, low], 0)
        product = lax.dot_general(stack, slab_stack, (((0,), (0,)), ((), ())), preferred_element_type=jnp.float32)
        rest = jnp.concatenate([one_ref[p, width:, :], two_ref[p, width:, :]], 1)
        targets_out[:, p * wide : (p + 1) * wide] = rest - jnp.dot(
            lead, solved, precision=HIGHEST, preferred_element_type=jnp.float32
        )
        loads[p].wait()
        held[p * wide : (p + 1) * wide, :] = held[p * wide : (p + 1) * wide, :] - product
        if p == 0:

            @pl.when(is_first)
            def _():
                held[:width, :] = slab_factor
                targets_out[:, :width] = lead

        stores[p].start()
    for store in stores:
        store.wait()


def update(first, one, two, inverse, down, panel, slab):
    count, depth, _ = one.shape
    width, wide = panel.shape
    vmem = pl.BlockSpec(memory_space=pltpu.VMEM)
    hbm = pl.BlockSpec(memory_space=pl.ANY)
    return pl.pallas_call(
        update_kernel,
        out_shape=(
            jax.ShapeDtypeStruct(slab.shape, jnp.float32),
            jax.ShapeDtypeStruct((depth - width, count * wide), jnp.float32),
            jax.ShapeDtypeStruct(panel.shape, jnp.float32),
        ),
        in_specs=[pl.BlockSpec(memory_space=pltpu.SMEM), vmem, vmem, vmem, vmem, vmem, hbm],
        out_specs=(hbm, vmem, vmem),
        scratch_shapes=[
            pltpu.VMEM(slab.shape, jnp.float32),
            pltpu.SemaphoreType.DMA((count,)),
            pltpu.SemaphoreType.DMA((count,)),
        ],
        compiler_params=pltpu.CompilerParams(vmem_limit_bytes=24 << 20),
        cost_estimate=pl.CostEstimate(
            flops=6 * slab.size * width, bytes_accessed=8 * slab.size, transcendentals=0
        ),
        name="update_slab",
    )(first, one, two, inverse, down, panel, slab)


def from_first(value, axis):
    size, index = lax.axis_size(axis), lax.axis_index(axis)
    reach = size
    while reach > 1:
        half = reach // 2
        pairs = [(i, i + half) for i in range(0, size, reach)]
        arrived = lax.ppermute(value, axis, pairs)
        value = jnp.where(index % reach == half, arrived, value)
        reach = half
    return value


def body(kernel_panel, kernel_slab, targets):
    width, wide = kernel_panel.shape
    cols = lax.axis_size("col")
    mine = targets.shape[0] // cols

    def exchange(lo, hi):
        pieces = jnp.broadcast_to(kernel_panel[None, :, lo:hi], (cols, width, hi - lo))
        sent = jnp.concatenate([pieces, targets[:, lo:hi].reshape(cols, mine, hi - lo)], 1)
        return sent

    sent_one, sent_two = exchange(0, LANES), exchange(LANES, wide)
    one = lax.all_to_all(sent_one, "col", split_axis=0, concat_axis=0)
    two = lax.all_to_all(sent_two, "col", split_axis=0, concat_axis=0)
    down = jnp.concatenate([one[0], kernel_slab[:width, :LANES], kernel_slab[:width, LANES:]], 0)
    down = from_first(down, "row")
    inverse = invert(down[:width], width)
    first = (lax.axis_index("row") == 0).astype(jnp.int32).reshape(1)
    return tuple(update(first, one, two, inverse, down, kernel_panel, kernel_slab))


def solution(mesh):
    in_specs = (P(None, ("row", "col")), P("row", "col"), P(None, ("row", "col")))
    out_specs = (P("row", "col"), P("col", "row"), P(None, ("row", "col")))
    return jax.shard_map(body, mesh=mesh, in_specs=in_specs, out_specs=out_specs, check_vma=False)
```

time: 90.6 us -> 62.2 us (0.69)
  the two profiles are of different devices: /device:TPU:24 before, /device:TPU:16 now
where the time goes in v2:
time: 62.2 us; the launch traced here: 61.5 us
  waiting for transfers between devices  24 us (39%)
  starting transfers between devices  15.4 us (25%)
  Pallas kernels  13.3 us (21%)
  local copies, waits for them, and re-layouts  6.24 us (10%)
  other arithmetic  1.82 us (3%)
  between operations  0.76 us (1%)
    all_to_all x1, waiting for transfers between devices, body(): one = lax.all_to_all(sent_one, 'col', split_axis=0, concat_axis=0)  12.2 us
    pallas_call x1, Pallas kernels, update(): pl.pallas_call(update_kernel, out_shape=(jax.ShapeDtypeStruct(slab.shape,...  9.57 us
    all_to_all x1, starting transfers between devices, body(): one = lax.all_to_all(sent_one, 'col', split_axis=0, concat_axis=0)  7.88 us
    ppermute x3, waiting for transfers between devices, from_first(): arrived = lax.ppermute(value, axis, pairs)  7.71 us
    all_to_all x1, waiting for transfers between devices, body(): two = lax.all_to_all(sent_two, 'col', split_axis=0, concat_axis=0)  4.19 us
    ppermute x3, starting transfers between devices, from_first(): arrived = lax.ppermute(value, axis, pairs)  3.88 us
    pallas_call x1, Pallas kernels, invert(): pl.pallas_call(invert_kernel, out_shape=jax.ShapeDtypeStruct((width, widt...  3.7 us
    all_to_all x1, starting transfers between devices, body(): two = lax.all_to_all(sent_two, 'col', split_axis=0, concat_axis=0)  3.59 us
  transfers between devices with their start and end apart: 5, of which 4 were waited for; matrix products, arithmetic and copies ran while one was open for 4% of the time, Pallas kernels for 6%

profile of v2, /device:TPU:16, one launch (start us, length us, event | category | flops | bytes accessed | tf_op | source)
XLA Modules:
  0.0 61.5 jit_solution(15258169564668211746)
XLA Ops:
  0.6 0.8 %fusion.2 = (f32[64,128]{1,0:T(8,128)S(1)}, f32[64,128]{1,0:T(8,128)S(1)}) fusion(f32[64,256]{1,0:T(8,128)} %panel_ref.1), kind=kLoop, calls=%fused_computation.9 | loop fusion | bytes 131072 | tf_op jit(solution)/shard_map/slice | solution.py:157
  1.4 0.0 copy-start.1
  1.4 1.0 %fusion.1 = (f32[256,128]{1,0:T(8,128)S(1)}, f32[256,128]{1,0:T(8,128)S(1)}) fusion(f32[256,256]{1,0:T(8,128)} %param.5), kind=kLoop, calls=%fused_computation.8 | loop fusion | bytes 524288 | tf_op jit(solution)/shard_map/slice | solution.py:158
  2.5 0.9 %pad_maximum_fusion = f32[16,80,128]{2,1,0:T(8,128)} fusion(f32[16,16,128]{2,1,0:T(8,128)S(1)} %bitcast.6, f32[16,64,128]{2,1,0:T(8,128)S(1)} %broadcast_in_dim.4), kind=kLoop, calls=%fused_computation | loop fusion | flops 163840 | bytes 1310720 | tf_op jit(solution)/shard_map/concatenate | solution.py:158
  3.4 7.9 %all-to-all-start = ((f32[16,80,128]{2,1,0:T(8,128)}), f32[16,80,128]{2,1,0:T(8,128)S(1)}, u32[]{:S(2)}, u32[]{:S(2)}) async-start(f32[16,80,128]{2,1,0:T(8,128)} %pad_maximum_fusion), calls=%async_computation | async-start | bytes 1310720 | tf_op jit(solution)/shard_map/all_to_all | solution.py:162
  11.3 0.8 %fusion = (f32[64,128]{1,0:T(8,128)S(1)}, f32[64,128]{1,0:T(8,128)S(1)}) fusion(f32[4096,256]{1,0:T(8,128)} %slab_ref.1), kind=kLoop, calls=%fused_computation.7 | loop fusion | bytes 131072 | tf_op jit(solution)/shard_map/slice | solution.py:164
  12.0 12.2 %all-to-all-done.one_ref = f32[16,80,128]{2,1,0:T(8,128)S(1)} async-done(((f32[16,80,128]{2,1,0:T(8,128)}), f32[16,80,128]{2,1,0:T(8,128)S(1)}, u32[]{:S(2)}, u32[]{:S(2)}) %all-to-all-start) | async-done | bytes 655392 | tf_op jit(solution)/shard_map/all_to_all | solution.py:162
  24.2 1.3 %collective-permute-start = (f32[208,128]{1,0:T(8,128)S(1)}, f32[208,128]{1,0:T(8,128)S(1)}, u32[]{:S(2)}, u32[]{:S(2)}) collective-permute-start(f32[208,128]{1,0:T(8,128)S(1)} %pad_maximum_fusion.2), channel_id=1, source_target_pairs={{0,64},{1,65},{2,66},{3,67},{4,68},{5,69},{6,70},{7,71},{8,72},{9,... | collective-permute-start | bytes 319496 | tf_op jit(solution)/shard_map/ppermute | solution.py:145
  25.5 6.8 %collective-permute-done = f32[208,128]{1,0:T(8,128)S(1)} collective-permute-done((f32[208,128]{1,0:T(8,128)S(1)}, f32[208,128]{1,0:T(8,128)S(1)}, u32[]{:S(2)}, u32[]{:S(2)}) %collective-permute-start) | collective-permute-done | bytes 106528 | tf_op jit(solution)/shard_map/ppermute | solution.py:145
  32.3 1.3 %collective-permute-start.1 = (f32[208,128]{1,0:T(8,128)S(1)}, f32[208,128]{1,0:T(8,128)S(1)}, u32[]{:S(2)}, u32[]{:S(2)}) collective-permute-start(f32[208,128]{1,0:T(8,128)S(1)} %broadcast_select_fusion), channel_id=1, source_target_pairs={{0,32},{64,96},{1,33},{65,97},{2,34},{66,98},{3,35},{67,99},{4,36}... | collective-permute-start | bytes 319496 | tf_op jit(solution)/shard_map/ppermute | solution.py:145
  33.7 0.9 %pad_maximum_fusion.1 = f32[16,80,128]{2,1,0:T(8,128)} fusion(f32[16,16,128]{2,1,0:T(8,128)S(1)} %bitcast.5, f32[16,64,128]{2,1,0:T(8,128)S(1)} %broadcast_in_dim.5), kind=kLoop, calls=%fused_computation.1 | loop fusion | flops 163840 | bytes 1310720 | tf_op jit(solution)/shard_map/concatenate | solution.py:158
  34.6 3.6 %all-to-all-start.1 = ((f32[16,80,128]{2,1,0:T(8,128)}), f32[16,80,128]{2,1,0:T(8,128)S(1)}, u32[]{:S(2)}, u32[]{:S(2)}) async-start(f32[16,80,128]{2,1,0:T(8,128)} %pad_maximum_fusion.1), calls=%async_computation.1 | async-start | bytes 1310720 | tf_op jit(solution)/shard_map/all_to_all | solution.py:163
  38.2 0.0 collective-permute-done.1
  38.2 1.3 %collective-permute-start.2 = (f32[208,128]{1,0:T(8,128)S(1)}, f32[208,128]{1,0:T(8,128)S(1)}, u32[]{:S(2)}, u32[]{:S(2)}) collective-permute-start(f32[208,128]{1,0:T(8,128)S(1)} %broadcast_select_fusion.1), channel_id=1, source_target_pairs={{0,16},{32,48},{64,80},{96,112},{1,17},{33,49},{65,81},{97,113},{2... | collective-permute-start | bytes 319496 | tf_op jit(solution)/shard_map/ppermute | solution.py:145
  39.5 0.9 %collective-permute-done.2 = f32[208,128]{1,0:T(8,128)S(1)} collective-permute-done((f32[208,128]{1,0:T(8,128)S(1)}, f32[208,128]{1,0:T(8,128)S(1)}, u32[]{:S(2)}, u32[]{:S(2)}) %collective-permute-start.2) | collective-permute-done | bytes 106528 | tf_op jit(solution)/shard_map/ppermute | solution.py:145
  40.5 0.6 %slice.33.lead_ref = f32[64,128]{1,0:T(8,128)} slice(f32[208,128]{1,0:T(8,128)S(1)} %broadcast_select_fusion.2.down_ref), slice={[0:64], [0:128]} | slice | bytes 65536 | tf_op jit(solution)/shard_map/slice | solution.py:166
  41.1 3.7 %invert_factor.1.inverse_ref = f32[64,64]{1,0:T(8,128)} custom-call(f32[64,128]{1,0:T(8,128)} %slice.33.lead_ref), custom_call_target="tpu_custom_call" | custom-call | flops 1048576 | bytes 32768 | tf_op jit(solution)/shard_map/invert_factor/pallas_call | solution.py:48
  44.8 4.2 %all-to-all-done.1.two_ref = f32[16,80,128]{2,1,0:T(8,128)S(1)} async-done(((f32[16,80,128]{2,1,0:T(8,128)}), f32[16,80,128]{2,1,0:T(8,128)S(1)}, u32[]{:S(2)}, u32[]{:S(2)}) %all-to-all-start.1) | async-done | bytes 655392 | tf_op jit(solution)/shard_map/all_to_all | solution.py:163
  49.0 0.0 copy-done.1
  49.0 0.0 copy-start
  49.0 2.2 %copy-done = f32[4096,256]{1,0:T(8,128)S(1)} copy-done((f32[4096,256]{1,0:T(8,128)S(1)}, f32[4096,256]{1,0:T(8,128)}, u32[]{:S(2)}) %copy-start) | copy-done | bytes 4194328
  51.2 0.0 copy-start.2
  51.2 0.8 %copy-done.2 = f32[64,64]{1,0:T(8,128)S(1)} copy-done((f32[64,64]{1,0:T(8,128)S(1)}, f32[64,64]{1,0:T(8,128)}, u32[]{:S(2)}) %copy-start.2) | copy-done | bytes 16408
  51.9 9.6 %update_slab.1 = (f32[4096,256]{1,0:T(8,128)}, f32[16,4096]{1,0:T(8,128)}, f32[64,256]{1,0:T(8,128)}) custom-call(s32[1]{0:T(128)} %bitcast.first_ref, f32[16,80,128]{2,1,0:T(8,128)S(1)} %all-to-all-done.one_ref, f32[16,80,128]{2,1,0:T(8,128)S(1)} %all-to-all-done.1.two_ref, f32[64,64]{1,0:T(8,128)S(1)} %copy-done.2, ...), custom_call_target="tpu_custom_call" | custom-call | flops 402653184 | bytes 8388608 | tf_op jit(solution)/shard_map/update_slab/pallas_call | solution.py:117
  (7 shorter events, 0.1 us)
Async XLA Ops:
  1.4 47.6 %copy-start.1 = (f32[64,256]{1,0:T(8,128)S(1)}, f32[64,256]{1,0:T(8,128)}, u32[]{:S(2)}) copy-start(f32[64,256]{1,0:T(8,128)} %panel_ref.1) | copy-start | bytes 196612
  3.4 20.8 %all-to-all-start = ((f32[16,80,128]{2,1,0:T(8,128)}), f32[16,80,128]{2,1,0:T(8,128)S(1)}, u32[]{:S(2)}, u32[]{:S(2)}) async-start(f32[16,80,128]{2,1,0:T(8,128)} %pad_maximum_fusion), calls=%async_computation | async-start | bytes 1310720 | tf_op jit(solution)/shard_map/all_to_all | solution.py:162
  24.2 8.1 %collective-permute-start = (f32[208,128]{1,0:T(8,128)S(1)}, f32[208,128]{1,0:T(8,128)S(1)}, u32[]{:S(2)}, u32[]{:S(2)}) collective-permute-start(f32[208,128]{1,0:T(8,128)S(1)} %pad_maximum_fusion.2), channel_id=1, source_target_pairs={{0,64},{1,65},{2,66},{3,67},{4,68},{5,69},{6,70},{7,71},{8,72},{9,... | collective-permute-start | bytes 319496 | tf_op jit(solution)/shard_map/ppermute | solution.py:145
  32.3 5.9 %collective-permute-start.1 = (f32[208,128]{1,0:T(8,128)S(1)}, f32[208,128]{1,0:T(8,128)S(1)}, u32[]{:S(2)}, u32[]{:S(2)}) collective-permute-start(f32[208,128]{1,0:T(8,128)S(1)} %broadcast_select_fusion), channel_id=1, source_target_pairs={{0,32},{64,96},{1,33},{65,97},{2,34},{66,98},{3,35},{67,99},{4,36}... | collective-permute-start | bytes 319496 | tf_op jit(solution)/shard_map/ppermute | solution.py:145
  34.6 14.4 %all-to-all-start.1 = ((f32[16,80,128]{2,1,0:T(8,128)}), f32[16,80,128]{2,1,0:T(8,128)S(1)}, u32[]{:S(2)}, u32[]{:S(2)}) async-start(f32[16,80,128]{2,1,0:T(8,128)} %pad_maximum_fusion.1), calls=%async_computation.1 | async-start | bytes 1310720 | tf_op jit(solution)/shard_map/all_to_all | solution.py:163
  38.2 2.2 %collective-permute-start.2 = (f32[208,128]{1,0:T(8,128)S(1)}, f32[208,128]{1,0:T(8,128)S(1)}, u32[]{:S(2)}, u32[]{:S(2)}) collective-permute-start(f32[208,128]{1,0:T(8,128)S(1)} %broadcast_select_fusion.1), channel_id=1, source_target_pairs={{0,16},{32,48},{64,80},{96,112},{1,17},{33,49},{65,81},{97,113},{2... | collective-permute-start | bytes 319496 | tf_op jit(solution)/shard_map/ppermute | solution.py:145
  49.0 2.2 %copy-start = (f32[4096,256]{1,0:T(8,128)S(1)}, f32[4096,256]{1,0:T(8,128)}, u32[]{:S(2)}) copy-start(f32[4096,256]{1,0:T(8,128)} %slab_ref.1) | copy-start | bytes 12582916
  51.2 0.8 %copy-start.2 = (f32[64,64]{1,0:T(8,128)S(1)}, f32[64,64]{1,0:T(8,128)}, u32[]{:S(2)}) copy-start(f32[64,64]{1,0:T(8,128)} %invert_factor.1.inverse_ref) | copy-start | bytes 49156

commit v3 on v2

v3 whole, which is shorter than its diff:
```python
import jax
import jax.numpy as jnp
from jax import lax
from jax.experimental import pallas as pl
from jax.experimental.pallas import tpu as pltpu
from jax.sharding import PartitionSpec as P

HIGHEST = lax.Precision.HIGHEST
LANES = 128
SUB = 8
GROUPS = 4


def dot(left, right, dims=((1,), (0,))):
    return lax.dot_general(left, right, (dims, ((), ())), preferred_element_type=jnp.float32)


def exact(left, right, dims=((1,), (0,))):
    return lax.dot_general(left, right, (dims, ((), ())), precision=HIGHEST, preferred_element_type=jnp.float32)


def halves(value):
    high = value.astype(jnp.bfloat16)
    return high, (value - high.astype(jnp.float32)).astype(jnp.bfloat16)


def thirds(value):
    high = value.astype(jnp.bfloat16)
    rest = value - high.astype(jnp.float32)
    return (high, *halves(rest))


def inverse_factor(corner, width):
    count = width // SUB
    shape = (SUB, LANES)
    lane = lax.broadcasted_iota(jnp.int32, shape, 1)
    row = lax.broadcasted_iota(jnp.int32, shape, 0)
    blocks = []
    for i in range(count):
        part = corner[i * SUB : (i + 1) * SUB]
        unit = jnp.where(lane - width == row + i * SUB, 1.0, 0.0).astype(jnp.float32)
        blocks.append(jnp.where(lane < width, part, unit))
    for b in range(count):
        below = range(b + 1, count)
        spread = [
            {i: jnp.broadcast_to(blocks[i][:, b * SUB + j : b * SUB + j + 1], shape) for i in range(b, count)}
            for j in range(SUB)
        ]
        for j in range(SUB):
            pivot = jnp.broadcast_to(spread[j][b][j : j + 1, :], shape)
            scale = lax.rsqrt(pivot)
            scale = scale * (1.5 - 0.5 * (pivot * scale) * scale)
            top = jnp.broadcast_to(blocks[b][j : j + 1, :], shape) * scale
            factor = {i: spread[j][i] * scale for i in below}
            factor[b] = jnp.where(row > j, spread[j][b] * scale, 0.0)
            for k in range(j + 1, SUB):
                entry = jnp.broadcast_to(spread[k][b][j : j + 1, :], shape) * scale
                for i in range(b, count):
                    spread[k][i] = spread[k][i] - factor[i] * entry
            blocks[b] = jnp.where(row == j, top, blocks[b] - factor[b] * top)
            for i in below:
                blocks[i] = blocks[i] - factor[i] * top
    return jnp.concatenate([block[:, width:] for block in blocks], 0)


def step_kernel(first_ref, got_ref, lead_ref, slab_panel_ref, panel_ref, slab_ref,
                slab_out, targets_out, factor_out, held, pieces, stacks, arrive, leave, brought):
    count, _, wide = pieces.shape
    width = panel_ref.shape[0]
    each = count // GROUPS
    loads, stores = [], []
    for g in range(GROUPS):
        rows = pl.ds(g * each * wide, each * wide)
        loads.append(pltpu.make_async_copy(slab_ref.at[rows], held.at[rows], arrive.at[g]))
        stores.append(pltpu.make_async_copy(held.at[rows], slab_out.at[rows], leave.at[g]))
    bring = pltpu.make_async_copy(got_ref, pieces, brought)
    bring.start()
    for load in loads:
        load.start()
    is_first = first_ref[0] == 1
    inverse = inverse_factor(lead_ref[:width, :], width)
    slab_factor = exact(inverse, slab_panel_ref[...])
    high, low = halves(slab_factor)
    slab_stack = jnp.concatenate([high, low, high], 0)
    high, middle, low = thirds(inverse)
    large = jnp.concatenate([high, high, middle, middle], 1)
    small = jnp.concatenate([high, low], 1)
    bring.wait()
    for p in range(count):
        one, two, three = thirds(pieces[p, :width, :])
        solved = dot(large, jnp.concatenate([one, two, one, two], 0))
        solved = solved + dot(small, jnp.concatenate([three, one], 0))
        high, low = halves(solved)
        stacks[:, p * wide : (p + 1) * wide] = jnp.concatenate([high, high, low], 0)
    for g in range(GROUPS):
        loads[g].wait()
        for p in range(g * each, (g + 1) * each):
            product = dot(stacks[:, p * wide : (p + 1) * wide], slab_stack, ((0,), (0,)))
            held[p * wide : (p + 1) * wide, :] = held[p * wide : (p + 1) * wide, :] - product
        if g == 0:

            @pl.when(is_first)
            def _():
                held[:width, :] = slab_factor

        stores[g].start()
    lead = exact(lead_ref[width:, :width], inverse, ((1,), (1,)))
    high, low = halves(lead)
    lead_stack = jnp.concatenate([high, low, high], 1)
    factor_out[...] = exact(inverse, panel_ref[...])
    for p in range(count):
        product = dot(lead_stack, stacks[:, p * wide : (p + 1) * wide])
        targets_out[:, p * wide : (p + 1) * wide] = pieces[p, width:, :] - product

    @pl.when(is_first)
    def _():
        targets_out[:, :width] = lead

    for store in stores:
        store.wait()


def step(first, got, lead, slab_panel, panel, slab):
    count, depth, wide = got.shape
    width = panel.shape[0]
    vmem = pl.BlockSpec(memory_space=pltpu.VMEM)
    hbm = pl.BlockSpec(memory_space=pl.ANY)
    return pl.pallas_call(
        step_kernel,
        out_shape=(
            jax.ShapeDtypeStruct(slab.shape, jnp.float32),
            jax.ShapeDtypeStruct((depth - width, count * wide), jnp.float32),
            jax.ShapeDtypeStruct(panel.shape, jnp.float32),
        ),
        in_specs=[pl.BlockSpec(memory_space=pltpu.SMEM), hbm, vmem, vmem, vmem, hbm],
        out_specs=(hbm, vmem, vmem),
        scratch_shapes=[
            pltpu.VMEM(slab.shape, jnp.float32),
            pltpu.VMEM(got.shape, jnp.float32),
            pltpu.VMEM((3 * width, count * wide), jnp.bfloat16),
            pltpu.SemaphoreType.DMA((GROUPS,)),
            pltpu.SemaphoreType.DMA((GROUPS,)),
            pltpu.SemaphoreType.DMA(()),
        ],
        compiler_params=pltpu.CompilerParams(vmem_limit_bytes=56 << 20),
        cost_estimate=pl.CostEstimate(
            flops=6 * slab.size * width, bytes_accessed=8 * slab.size, transcendentals=width
        ),
        name="factor_and_update",
    )(first, got, lead, slab_panel, panel, slab)


def from_first(value, axis):
    size, index = lax.axis_size(axis), lax.axis_index(axis)
    reach = size
    while reach > 1:
        half = reach // 2
        pairs = [(i, i + half) for i in range(0, size, reach)]
        arrived = lax.ppermute(value, axis, pairs)
        value = jnp.where(index % reach == half, arrived, value)
        reach = half
    return value


def body(kernel_panel, kernel_slab, targets):
    width, wide = kernel_panel.shape
    cols = lax.axis_size("col")
    mine = targets.shape[0] // cols
    pieces = jnp.broadcast_to(kernel_panel[None], (cols, width, wide))
    sent = jnp.concatenate([pieces, targets.reshape(cols, mine, wide)], 1)
    got = lax.all_to_all(sent, "col", split_axis=0, concat_axis=0)
    slab_panel = from_first(kernel_slab[:width], "row")
    lead, slab_panel = lax.optimization_barrier((got[0, :, :LANES], slab_panel))
    lead = from_first(lead, "row")
    first = (lax.axis_index("row") == 0).astype(jnp.int32).reshape(1)
    return tuple(step(first, got, lead, slab_panel, kernel_panel, kernel_slab))


def solution(mesh):
    in_specs = (P(None, ("row", "col")), P("row", "col"), P(None, ("row", "col")))
    out_specs = (P("row", "col"), P("col", "row"), P(None, ("row", "col")))
    return jax.shard_map(body, mesh=mesh, in_specs=in_specs, out_specs=out_specs, check_vma=False)
```

time: 62.2 us -> 56.6 us (0.910)
  the two profiles are of different devices: /device:TPU:16 before, /device:TPU:24 now
where the time goes in v3:
time: 56.6 us; the launch traced here: 55.6 us
  waiting for transfers between devices  25.4 us (45%)
  starting transfers between devices  14.3 us (25%)
  Pallas kernels  9 us (16%)
  other arithmetic  4.25 us (8%)
  local copies, waits for them, and re-layouts  1.79 us (3%)
  between operations  0.77 us (1%)
    ppermute x6, waiting for transfers between devices, from_first(): arrived = lax.ppermute(value, axis, pairs)  21 us
    pallas_call x1, Pallas kernels, step(): pl.pallas_call(step_kernel, out_shape=(jax.ShapeDtypeStruct(slab.shape, j...  9 us
    all_to_all x1, starting transfers between devices, body(): got = lax.all_to_all(sent, 'col', split_axis=0, concat_axis=0)  7.88 us
    ppermute x6, starting transfers between devices, from_first(): arrived = lax.ppermute(value, axis, pairs)  6.46 us
    all_to_all x1, waiting for transfers between devices, body(): got = lax.all_to_all(sent, 'col', split_axis=0, concat_axis=0)  4.38 us
    concatenate x1, other arithmetic, body(): sent = jnp.concatenate([pieces, targets.reshape(cols, mine, wide)], 1)  2.13 us
    select_n x6, other arithmetic, from_first(): value = jnp.where(index % reach == half, arrived, value)  2.12 us
  transfers between devices with their start and end apart: 7, of which 5 were waited for; matrix products, arithmetic and copies ran while one was open for 4% of the time, Pallas kernels for 0%

profile of v3, /device:TPU:24, one launch (start us, length us, event | category | flops | bytes accessed | tf_op | source)
XLA Modules:
  0.0 55.6 jit_solution(15141993488806205942)
XLA Ops:
  0.6 0.9 %broadcast_in_dim.2 = f32[16,64,256]{2,1,0:T(8,128)S(1)} broadcast(f32[64,256]{1,0:T(8,128)} %panel_ref.1), dimensions={1,2} | broadcast | bytes 1114112 | tf_op jit(solution)/shard_map/broadcast_in_dim | solution.py:169
  1.6 2.1 %pad_maximum_fusion = f32[16,80,256]{2,1,0:T(8,128)} fusion(f32[16,16,256]{2,1,0:T(8,128)} %bitcast.4, f32[16,64,256]{2,1,0:T(8,128)S(1)} %broadcast_in_dim.2), kind=kLoop, calls=%fused_computation | loop fusion | flops 327680 | bytes 2621440 | tf_op jit(solution)/shard_map/concatenate | solution.py:170
  3.7 7.9 %all-to-all-start = ((f32[16,80,256]{2,1,0:T(8,128)}), f32[16,80,256]{2,1,0:T(8,128)S(1)}, u32[]{:S(2)}, u32[]{:S(2)}) async-start(f32[16,80,256]{2,1,0:T(8,128)} %pad_maximum_fusion), calls=%async_computation | async-start | bytes 2621440 | tf_op jit(solution)/shard_map/all_to_all | solution.py:171
  11.6 0.8 %slice.7 = f32[64,256]{1,0:T(8,128)S(1)} slice(f32[4096,256]{1,0:T(8,128)} %slab_ref.1), slice={[0:64], [0:256]} | slice | bytes 131072 | tf_op jit(solution)/shard_map/slice | solution.py:172
  12.4 0.7 %collective-permute-start = (f32[64,256]{1,0:T(8,128)S(1)}, f32[64,256]{1,0:T(8,128)S(1)}, u32[]{:S(2)}, u32[]{:S(2)}) collective-permute-start(f32[64,256]{1,0:T(8,128)S(1)} %slice.7), channel_id=1, source_target_pairs={{0,64},{1,65},{2,66},{3,67},{4,68},{5,69},{6,70},{7,71},{8,72},{9,... | collective-permute-start | bytes 196616 | tf_op jit(solution)/shard_map/ppermute | solution.py:159
  13.1 0.0 collective-permute-done
  13.1 0.9 %broadcast_select_fusion = f32[64,256]{1,0:T(8,128)S(1)} fusion(f32[64,256]{1,0:T(8,128)S(1)} %collective-permute-done, pred[]{:T(512)S(6)} %eq.25, f32[4096,256]{1,0:T(8,128)} %slab_ref.1), kind=kLoop, calls=%fused_computation.2 | loop fusion | flops 16384 | bytes 196609 | tf_op jit(solution)/shard_map/jit(_where)/select_n | solution.py:160
  14.0 1.3 %collective-permute-start.1 = (f32[64,256]{1,0:T(8,128)S(1)}, f32[64,256]{1,0:T(8,128)S(1)}, u32[]{:S(2)}, u32[]{:S(2)}) collective-permute-start(f32[64,256]{1,0:T(8,128)S(1)} %broadcast_select_fusion), channel_id=1, source_target_pairs={{0,32},{64,96},{1,33},{65,97},{2,34},{66,98},{3,35},{67,99},{4,36}... | collective-permute-start | bytes 196616 | tf_op jit(solution)/shard_map/ppermute | solution.py:159
  15.3 9.9 %collective-permute-done.1 = f32[64,256]{1,0:T(8,128)S(1)} collective-permute-done((f32[64,256]{1,0:T(8,128)S(1)}, f32[64,256]{1,0:T(8,128)S(1)}, u32[]{:S(2)}, u32[]{:S(2)}) %collective-permute-start.1) | collective-permute-done | bytes 65568 | tf_op jit(solution)/shard_map/ppermute | solution.py:159
  25.2 1.3 %collective-permute-start.2 = (f32[64,256]{1,0:T(8,128)S(1)}, f32[64,256]{1,0:T(8,128)S(1)}, u32[]{:S(2)}, u32[]{:S(2)}) collective-permute-start(f32[64,256]{1,0:T(8,128)S(1)} %broadcast_select_fusion.1), channel_id=1, source_target_pairs={{0,16},{32,48},{64,80},{96,112},{1,17},{33,49},{65,81},{97,113},{2... | collective-permute-start | bytes 196616 | tf_op jit(solution)/shard_map/ppermute | solution.py:159
  26.5 0.9 %collective-permute-done.2 = f32[64,256]{1,0:T(8,128)S(1)} collective-permute-done((f32[64,256]{1,0:T(8,128)S(1)}, f32[64,256]{1,0:T(8,128)S(1)}, u32[]{:S(2)}, u32[]{:S(2)}) %collective-permute-start.2) | collective-permute-done | bytes 65568 | tf_op jit(solution)/shard_map/ppermute | solution.py:159
  27.4 0.6 %broadcast_select_fusion.2.slab_panel_ref = f32[64,256]{1,0:T(8,128)} fusion(f32[64,256]{1,0:T(8,128)S(1)} %collective-permute-done.2, f32[64,256]{1,0:T(8,128)S(1)} %broadcast_select_fusion.1, pred[]{:T(512)S(6)} %eq.23), kind=kLoop, calls=%fused_computation.4 | loop fusion | flops 16384 | bytes 196609 | tf_op jit(solution)/shard_map/jit(_where)/select_n | solution.py:160
  28.0 4.4 %all-to-all-done.got_ref = f32[16,80,256]{2,1,0:T(8,128)S(1)} async-done(((f32[16,80,256]{2,1,0:T(8,128)}), f32[16,80,256]{2,1,0:T(8,128)S(1)}, u32[]{:S(2)}, u32[]{:S(2)}) %all-to-all-start) | async-done | bytes 1310752 | tf_op jit(solution)/shard_map/all_to_all | solution.py:171
  32.4 0.0 copy-start
  32.4 0.7 %collective-permute-start.3 = (f32[80,128]{1,0:T(8,128)S(1)}, f32[80,128]{1,0:T(8,128)S(1)}, u32[]{:S(2)}, u32[]{:S(2)}) collective-permute-start(f32[80,128]{1,0:T(8,128)S(1)} %slice_bitcast_fusion), channel_id=1, source_target_pairs={{0,64},{1,65},{2,66},{3,67},{4,68},{5,69},{6,70},{7,71},{8,72},{9,... | collective-permute-start | bytes 122888 | tf_op jit(solution)/shard_map/ppermute | solution.py:159
  33.1 0.0 collective-permute-done.3
  33.1 1.3 %collective-permute-start.4 = (f32[80,128]{1,0:T(8,128)S(1)}, f32[80,128]{1,0:T(8,128)S(1)}, u32[]{:S(2)}, u32[]{:S(2)}) collective-permute-start(f32[80,128]{1,0:T(8,128)S(1)} %broadcast_select_fusion.3), channel_id=1, source_target_pairs={{0,32},{64,96},{1,33},{65,97},{2,34},{66,98},{3,35},{67,99},{4,36}... | collective-permute-start | bytes 122888 | tf_op jit(solution)/shard_map/ppermute | solution.py:159
  34.4 9.4 %collective-permute-done.4 = f32[80,128]{1,0:T(8,128)S(1)} collective-permute-done((f32[80,128]{1,0:T(8,128)S(1)}, f32[80,128]{1,0:T(8,128)S(1)}, u32[]{:S(2)}, u32[]{:S(2)}) %collective-permute-start.4) | collective-permute-done | bytes 40992 | tf_op jit(solution)/shard_map/ppermute | solution.py:159
  43.8 1.3 %collective-permute-start.5 = (f32[80,128]{1,0:T(8,128)S(1)}, f32[80,128]{1,0:T(8,128)S(1)}, u32[]{:S(2)}, u32[]{:S(2)}) collective-permute-start(f32[80,128]{1,0:T(8,128)S(1)} %broadcast_select_fusion.4), channel_id=1, source_target_pairs={{0,16},{32,48},{64,80},{96,112},{1,17},{33,49},{65,81},{97,113},{2... | collective-permute-start | bytes 122888 | tf_op jit(solution)/shard_map/ppermute | solution.py:159
  45.1 0.8 %collective-permute-done.5 = f32[80,128]{1,0:T(8,128)S(1)} collective-permute-done((f32[80,128]{1,0:T(8,128)S(1)}, f32[80,128]{1,0:T(8,128)S(1)}, u32[]{:S(2)}, u32[]{:S(2)}) %collective-permute-start.5) | collective-permute-done | bytes 40992 | tf_op jit(solution)/shard_map/ppermute | solution.py:159
  45.9 0.6 %broadcast_select_fusion.5.lead_ref = f32[80,128]{1,0:T(8,128)} fusion(f32[80,128]{1,0:T(8,128)S(1)} %collective-permute-done.5, f32[80,128]{1,0:T(8,128)S(1)} %broadcast_select_fusion.4, pred[]{:T(512)S(6)} %eq.23), kind=kLoop, calls=%fused_computation.7 | loop fusion | flops 10240 | bytes 122881 | tf_op jit(solution)/shard_map/jit(_where)/select_n | solution.py:160
  46.6 0.0 copy-done
  46.6 9.0 %factor_and_update.1 = (f32[4096,256]{1,0:T(8,128)}, f32[16,4096]{1,0:T(8,128)}, f32[64,256]{1,0:T(8,128)}) custom-call(s32[1]{0:T(128)} %bitcast.first_ref, f32[16,80,256]{2,1,0:T(8,128)} %copy-done, f32[80,128]{1,0:T(8,128)} %broadcast_select_fusion.5.lead_ref, f32[64,256]{1,0:T(8,128)} %broadcast_select_fusion.2.slab_panel_ref, f32[64,256]{1,0:T(8,128)} %panel_ref.1, ...), custom_call_target="tpu_custom_call" | custom-call | flops 402653184 | bytes 8388608 | tf_op jit(solution)/shard_map/factor_and_update/pallas_call | solution.py:128
  (4 shorter events, 0.0 us)
Async XLA Ops:
  3.7 28.7 %all-to-all-start = ((f32[16,80,256]{2,1,0:T(8,128)}), f32[16,80,256]{2,1,0:T(8,128)S(1)}, u32[]{:S(2)}, u32[]{:S(2)}) async-start(f32[16,80,256]{2,1,0:T(8,128)} %pad_maximum_fusion), calls=%async_computation | async-start | bytes 2621440 | tf_op jit(solution)/shard_map/all_to_all | solution.py:171
  12.4 0.7 %collective-permute-start = (f32[64,256]{1,0:T(8,128)S(1)}, f32[64,256]{1,0:T(8,128)S(1)}, u32[]{:S(2)}, u32[]{:S(2)}) collective-permute-start(f32[64,256]{1,0:T(8,128)S(1)} %slice.7), channel_id=1, source_target_pairs={{0,64},{1,65},{2,66},{3,67},{4,68},{5,69},{6,70},{7,71},{8,72},{9,... | collective-permute-start | bytes 196616 | tf_op jit(solution)/shard_map/ppermute | solution.py:159
  14.0 11.2 %collective-permute-start.1 = (f32[64,256]{1,0:T(8,128)S(1)}, f32[64,256]{1,0:T(8,128)S(1)}, u32[]{:S(2)}, u32[]{:S(2)}) collective-permute-start(f32[64,256]{1,0:T(8,128)S(1)} %broadcast_select_fusion), channel_id=1, source_target_pairs={{0,32},{64,96},{1,33},{65,97},{2,34},{66,98},{3,35},{67,99},{4,36}... | collective-permute-start | bytes 196616 | tf_op jit(solution)/shard_map/ppermute | solution.py:159
  25.2 2.2 %collective-permute-start.2 = (f32[64,256]{1,0:T(8,128)S(1)}, f32[64,256]{1,0:T(8,128)S(1)}, u32[]{:S(2)}, u32[]{:S(2)}) collective-permute-start(f32[64,256]{1,0:T(8,128)S(1)} %broadcast_select_fusion.1), channel_id=1, source_target_pairs={{0,16},{32,48},{64,80},{96,112},{1,17},{33,49},{65,81},{97,113},{2... | collective-permute-start | bytes 196616 | tf_op jit(solution)/shard_map/ppermute | solution.py:159
  32.4 14.2 %copy-start = (f32[16,80,256]{2,1,0:T(8,128)}, f32[16,80,256]{2,1,0:T(8,128)S(1)}, u32[]{:S(2)}) copy-start(f32[16,80,256]{2,1,0:T(8,128)S(1)} %all-to-all-done.got_ref) | copy-start | bytes 3932164
  32.4 0.7 %collective-permute-start.3 = (f32[80,128]{1,0:T(8,128)S(1)}, f32[80,128]{1,0:T(8,128)S(1)}, u32[]{:S(2)}, u32[]{:S(2)}) collective-permute-start(f32[80,128]{1,0:T(8,128)S(1)} %slice_bitcast_fusion), channel_id=1, source_target_pairs={{0,64},{1,65},{2,66},{3,67},{4,68},{5,69},{6,70},{7,71},{8,72},{9,... | collective-permute-start | bytes 122888 | tf_op jit(solution)/shard_map/ppermute | solution.py:159
  33.1 10.7 %collective-permute-start.4 = (f32[80,128]{1,0:T(8,128)S(1)}, f32[80,128]{1,0:T(8,128)S(1)}, u32[]{:S(2)}, u32[]{:S(2)}) collective-permute-start(f32[80,128]{1,0:T(8,128)S(1)} %broadcast_select_fusion.3), channel_id=1, source_target_pairs={{0,32},{64,96},{1,33},{65,97},{2,34},{66,98},{3,35},{67,99},{4,36}... | collective-permute-start | bytes 122888 | tf_op jit(solution)/shard_map/ppermute | solution.py:159
  43.8 2.1 %collective-permute-start.5 = (f32[80,128]{1,0:T(8,128)S(1)}, f32[80,128]{1,0:T(8,128)S(1)}, u32[]{:S(2)}, u32[]{:S(2)}) collective-permute-start(f32[80,128]{1,0:T(8,128)S(1)} %broadcast_select_fusion.4), channel_id=1, source_target_pairs={{0,16},{32,48},{64,80},{96,112},{1,17},{33,49},{65,81},{97,113},{2... | collective-permute-start | bytes 122888 | tf_op jit(solution)/shard_map/ppermute | solution.py:159

commit v4 on v3

--- a/solution.py
+++ b/solution.py
@@ -63,8 +63,27 @@
     return jnp.concatenate([block[:, width:] for block in blocks], 0)
 
 
-def step_kernel(first_ref, got_ref, lead_ref, slab_panel_ref, panel_ref, slab_ref,
-                slab_out, targets_out, factor_out, held, pieces, stacks, arrive, leave, brought):
+def pack_kernel(panel_ref, targets_ref, sent_ref):
+    width = panel_ref.shape[0]
+    for p in range(sent_ref.shape[0]):
+        sent_ref[p, :width, :] = panel_ref[...]
+        sent_ref[p, width:, :] = targets_ref[p]
+
+
+def pack(panel, targets):
+    count, mine, wide = targets.shape
+    vmem = pl.BlockSpec(memory_space=pltpu.VMEM)
+    return pl.pallas_call(
+        pack_kernel,
+        out_shape=jax.ShapeDtypeStruct((count, panel.shape[0] + mine, wide), jnp.float32),
+        in_specs=[vmem, vmem],
+        out_specs=vmem,
+        name="pack_pieces",
+    )(panel, targets)
+
+
+def step_kernel(place_ref, pieces, kept_ref, arrived_ref, slab_panel_ref, panel_ref, slab_ref,
+                slab_out, targets_out, factor_out, held, stacks, solved_targets, own_factor, arrive, leave, end):
     count, _, wide = pieces.shape
     width = panel_ref.shape[0]
     each = count // GROUPS
@@ -73,19 +92,19 @@
         rows = pl.ds(g * each * wide, each * wide)
         loads.append(pltpu.make_async_copy(slab_ref.at[rows], held.at[rows], arrive.at[g]))
         stores.append(pltpu.make_async_copy(held.at[rows], slab_out.at[rows], leave.at[g]))
-    bring = pltpu.make_async_copy(got_ref, pieces, brought)
-    bring.start()
+    stores.append(pltpu.make_async_copy(own_factor, factor_out, end.at[0]))
+    stores.append(pltpu.make_async_copy(solved_targets, targets_out, end.at[1]))
     for load in loads:
         load.start()
-    is_first = first_ref[0] == 1
-    inverse = inverse_factor(lead_ref[:width, :], width)
+    is_first = place_ref[0] == 1
+    lead_rows = jnp.where(place_ref[1] == 1, arrived_ref[...], kept_ref[...])
+    inverse = inverse_factor(lead_rows[:width], width)
     slab_factor = exact(inverse, slab_panel_ref[...])
     high, low = halves(slab_factor)
     slab_stack = jnp.concatenate([high, low, high], 0)
     high, middle, low = thirds(inverse)
     large = jnp.concatenate([high, high, middle, middle], 1)
     small = jnp.concatenate([high, low], 1)
-    bring.wait()
     for p in range(count):
         one, two, three = thirds(pieces[p, :width, :])
         solved = dot(large, jnp.concatenate([one, two, one, two], 0))
@@ -104,76 +123,80 @@
                 held[:width, :] = slab_factor
 
         stores[g].start()
-    lead = exact(lead_ref[width:, :width], inverse, ((1,), (1,)))
+    own_factor[...] = exact(inverse, panel_ref[...])
+    stores[GROUPS].start()
+    lead = exact(lead_rows[width:, :width], inverse, ((1,), (1,)))
     high, low = halves(lead)
     lead_stack = jnp.concatenate([high, low, high], 1)
-    factor_out[...] = exact(inverse, panel_ref[...])
     for p in range(count):
         product = dot(lead_stack, stacks[:, p * wide : (p + 1) * wide])
-        targets_out[:, p * wide : (p + 1) * wide] = pieces[p, width:, :] - product
+        solved_targets[:, p * wide : (p + 1) * wide] = pieces[p, width:, :] - product
 
     @pl.when(is_first)
     def _():
-        targets_out[:, :width] = lead
-
+        solved_targets[:, :width] = lead
+
+    stores[GROUPS + 1].start()
     for store in stores:
         store.wait()
 
 
-def step(first, got, lead, slab_panel, panel, slab):
+def step(place, got, kept, arrived, slab_panel, panel, slab):
     count, depth, wide = got.shape
     width = panel.shape[0]
     vmem = pl.BlockSpec(memory_space=pltpu.VMEM)
     hbm = pl.BlockSpec(memory_space=pl.ANY)
+    outputs = (
+        jax.ShapeDtypeStruct(slab.shape, jnp.float32),
+        jax.ShapeDtypeStruct((depth - width, count * wide), jnp.float32),
+        jax.ShapeDtypeStruct(panel.shape, jnp.float32),
+    )
     return pl.pallas_call(
         step_kernel,
-        out_shape=(
-            jax.ShapeDtypeStruct(slab.shape, jnp.float32),
-            jax.ShapeDtypeStruct((depth - width, count * wide), jnp.float32),
-            jax.ShapeDtypeStruct(panel.shape, jnp.float32),
-        ),
-        in_specs=[pl.BlockSpec(memory_space=pltpu.SMEM), hbm, vmem, vmem, vmem, hbm],
-        out_specs=(hbm, vmem, vmem),
+        out_shape=outputs,
+        in_specs=[pl.BlockSpec(memory_space=pltpu.SMEM), vmem, vmem, vmem, vmem, vmem, hbm],
+        out_specs=(hbm, hbm, hbm),
         scratch_shapes=[
             pltpu.VMEM(slab.shape, jnp.float32),
-            pltpu.VMEM(got.shape, jnp.float32),
             pltpu.VMEM((3 * width, count * wide), jnp.bfloat16),
+            pltpu.VMEM(outputs[1].shape, jnp.float32),
+            pltpu.VMEM(panel.shape, jnp.float32),
             pltpu.SemaphoreType.DMA((GROUPS,)),
             pltpu.SemaphoreType.DMA((GROUPS,)),
-            pltpu.SemaphoreType.DMA(()),
+            pltpu.SemaphoreType.DMA((2,)),
         ],
-        compiler_params=pltpu.CompilerParams(vmem_limit_bytes=56 << 20),
+        compiler_params=pltpu.CompilerParams(vmem_limit_bytes=52 << 20),
         cost_estimate=pl.CostEstimate(
             flops=6 * slab.size * width, bytes_accessed=8 * slab.size, transcendentals=width
         ),
         name="factor_and_update",
-    )(first, got, lead, slab_panel, panel, slab)
-
-
-def from_first(value, axis):
-    size, index = lax.axis_size(axis), lax.axis_index(axis)
-    reach = size
-    while reach > 1:
-        half = reach // 2
-        pairs = [(i, i + half) for i in range(0, size, reach)]
-        arrived = lax.ppermute(value, axis, pairs)
-        value = jnp.where(index % reach == half, arrived, value)
-        reach = half
-    return value
+    )(place, got, kept, arrived, slab_panel, panel, slab)
 
 
 def body(kernel_panel, kernel_slab, targets):
     width, wide = kernel_panel.shape
-    cols = lax.axis_size("col")
+    rows, cols = lax.axis_size("row"), lax.axis_size("col")
+    row_index = lax.axis_index("row")
     mine = targets.shape[0] // cols
-    pieces = jnp.broadcast_to(kernel_panel[None], (cols, width, wide))
-    sent = jnp.concatenate([pieces, targets.reshape(cols, mine, wide)], 1)
+
+    def down(value):
+        reach = 1
+        while True:
+            arrived = lax.ppermute(value, "row", [(i, i + reach) for i in range(reach)])
+            new = (row_index >= reach) & (row_index < 2 * reach)
+            reach = 2 * reach
+            if reach == rows:
+                return value, arrived, new
+            value = jnp.where(new, arrived, value)
+
+    sent = pack(kernel_panel, targets.reshape(cols, mine, wide))
     got = lax.all_to_all(sent, "col", split_axis=0, concat_axis=0)
-    slab_panel = from_first(kernel_slab[:width], "row")
+    kept, arrived, new = down(kernel_slab[:width])
+    slab_panel = jnp.where(new, arrived, kept)
     lead, slab_panel = lax.optimization_barrier((got[0, :, :LANES], slab_panel))
-    lead = from_first(lead, "row")
-    first = (lax.axis_index("row") == 0).astype(jnp.int32).reshape(1)
-    return tuple(step(first, got, lead, slab_panel, kernel_panel, kernel_slab))
+    kept, arrived, new = down(lead)
+    place = jnp.stack([row_index == 0, new]).astype(jnp.int32)
+    return tuple(step(place, got, kept, arrived, slab_panel, kernel_panel, kernel_slab))
 
 
 def solution(mesh):

time: 56.6 us -> 49.3 us (0.87); the launches traced: 55.6 us -> 48.9 us
  other arithmetic: 4.25 us -> 0.97 us
  starting transfers between devices: 14.3 us -> 13.1 us
  local copies, waits for them, and re-layouts: 1.79 us -> 0.85 us
  waiting for transfers between devices: 25.4 us -> 24.7 us
  Pallas kernels: 9 us -> 8.43 us
    ppermute x6, waiting for transfers between devices: 21 us -> 17.2 us  [down(): arrived = lax.ppermute(value, 'row', [(i, i + reach) for i in range(reach)])]
    all_to_all x1, waiting for transfers between devices: 4.38 us -> 7.5 us  [body(): got = lax.all_to_all(sent, 'col', split_axis=0, concat_axis=0)]
    concatenate x1 -> x0, other arithmetic: 2.13 us -> none  [body(): sent = jnp.concatenate([pieces, targets.reshape(cols, mine, wide)], 1)]
    ppermute x6, starting transfers between devices: 6.46 us -> 5.21 us  [down(): arrived = lax.ppermute(value, 'row', [(i, i + reach) for i in range(reach)])]
    select_n x6 -> x5, other arithmetic: 2.12 us -> 0.89 us  [the longest x4 0.88 us: down(): value = jnp.where(new, arrived, value)]
    broadcast_in_dim x1 -> x0, local copies, waits for them, and re-layouts: 0.93 us -> none  [body(): pieces = jnp.broadcast_to(kernel_panel[None], (cols, width, wide))]
    pallas_call x1 -> x2, Pallas kernels: 9 us -> 8.43 us  [the longest x1 6.27 us: step(): pl.pallas_call(step_kernel, out_shape=outputs, in_specs=[pl.BlockSpec(mem...]
  transfers between devices with their start and end apart: 7 -> 7, of which waited for: 5 -> 3; matrix products, arithmetic and copies ran while one was open for 4% -> 4% of each run, Pallas kernels for 0% -> 0%
where the time goes in v4:
time: 49.3 us; the launch traced here: 48.9 us
  waiting for transfers between devices  24.7 us (50%)
  starting transfers between devices  13.1 us (27%)
  Pallas kernels  8.43 us (17%)
  other arithmetic  0.97 us (2%)
  local copies, waits for them, and re-layouts  0.85 us (2%)
  between operations  0.79 us (2%)
    ppermute x6, waiting for transfers between devices, down(): arrived = lax.ppermute(value, 'row', [(i, i + reach) for i in range(reach)])  17.2 us
    all_to_all x1, starting transfers between devices, body(): got = lax.all_to_all(sent, 'col', split_axis=0, concat_axis=0)  7.88 us
    all_to_all x1, waiting for transfers between devices, body(): got = lax.all_to_all(sent, 'col', split_axis=0, concat_axis=0)  7.5 us
    pallas_call x1, Pallas kernels, step(): pl.pallas_call(step_kernel, out_shape=outputs, in_specs=[pl.BlockSpec(mem...  6.27 us
    ppermute x6, starting transfers between devices, down(): arrived = lax.ppermute(value, 'row', [(i, i + reach) for i in range(reach)])  5.21 us
    pallas_call x1, Pallas kernels, pack(): pl.pallas_call(pack_kernel, out_shape=jax.ShapeDtypeStruct((count, panel....  2.16 us
  transfers between devices with their start and end apart: 7, of which 3 were waited for; matrix products, arithmetic and copies ran while one was open for 4% of the time, Pallas kernels for 0%

profile of v4, /device:TPU:24, one launch (start us, length us, event | category | flops | bytes accessed | tf_op | source)
XLA Modules:
  0.0 48.9 jit_solution(3658475062091608080)
XLA Ops:
  0.6 0.0 copy-start
  0.6 2.2 %pack_pieces.1 = f32[16,80,256]{2,1,0:T(8,128)} custom-call(f32[64,256]{1,0:T(8,128)} %panel_ref.3, f32[16,16,256]{2,1,0:T(8,128)} %bitcast.5), custom_call_target="tpu_custom_call" | custom-call | tf_op jit(solution)/shard_map/pack_pieces/pallas_call | solution.py:76
  2.8 7.9 %all-to-all-start = ((f32[16,80,256]{2,1,0:T(8,128)}), f32[16,80,256]{2,1,0:T(8,128)S(1)}, u32[]{:S(2)}, u32[]{:S(2)}) async-start(f32[16,80,256]{2,1,0:T(8,128)} %pack_pieces.1), calls=%async_computation | async-start | bytes 2621440 | tf_op jit(solution)/shard_map/all_to_all | solution.py:193
  10.7 0.8 %slice.7 = f32[64,256]{1,0:T(8,128)S(1)} slice(f32[4096,256]{1,0:T(8,128)} %slab_ref.1), slice={[0:64], [0:256]} | slice | bytes 131072 | tf_op jit(solution)/shard_map/slice | solution.py:194
  11.5 0.7 %collective-permute-start = (f32[64,256]{1,0:T(8,128)S(1)}, f32[64,256]{1,0:T(8,128)S(1)}, u32[]{:S(2)}, u32[]{:S(2)}) collective-permute-start(f32[64,256]{1,0:T(8,128)S(1)} %slice.7), channel_id=1, source_target_pairs={{0,16},{1,17},{2,18},{3,19},{4,20},{5,21},{6,22},{7,23},{8,24},{9,... | collective-permute-start | bytes 196616 | tf_op jit(solution)/shard_map/ppermute | solution.py:185
  12.2 0.0 collective-permute-done
  12.2 0.9 %broadcast_select_fusion = f32[64,256]{1,0:T(8,128)S(1)} fusion(f32[64,256]{1,0:T(8,128)S(1)} %collective-permute-done, pred[]{:T(512)S(6)} %and.15, f32[4096,256]{1,0:T(8,128)} %slab_ref.1), kind=kLoop, calls=%fused_computation.1 | loop fusion | flops 16384 | bytes 196609 | tf_op jit(solution)/shard_map/jit(_where)/select_n | solution.py:190
  13.1 0.7 %collective-permute-start.1 = (f32[64,256]{1,0:T(8,128)S(1)}, f32[64,256]{1,0:T(8,128)S(1)}, u32[]{:S(2)}, u32[]{:S(2)}) collective-permute-start(f32[64,256]{1,0:T(8,128)S(1)} %broadcast_select_fusion), channel_id=1, source_target_pairs={{0,32},{16,48},{1,33},{17,49},{2,34},{18,50},{3,35},{19,51},{4,36}... | collective-permute-start | bytes 196616 | tf_op jit(solution)/shard_map/ppermute | solution.py:185
  13.7 0.0 collective-permute-done.1
  13.8 1.3 %collective-permute-start.2 = (f32[64,256]{1,0:T(8,128)S(1)}, f32[64,256]{1,0:T(8,128)S(1)}, u32[]{:S(2)}, u32[]{:S(2)}) collective-permute-start(f32[64,256]{1,0:T(8,128)S(1)} %broadcast_select_fusion.1), channel_id=1, source_target_pairs={{0,64},{16,80},{32,96},{48,112},{1,65},{17,81},{33,97},{49,113},{2... | collective-permute-start | bytes 196616 | tf_op jit(solution)/shard_map/ppermute | solution.py:185
  15.1 8.9 %collective-permute-done.2 = f32[64,256]{1,0:T(8,128)S(1)} collective-permute-done((f32[64,256]{1,0:T(8,128)S(1)}, f32[64,256]{1,0:T(8,128)S(1)}, u32[]{:S(2)}, u32[]{:S(2)}) %collective-permute-start.2) | collective-permute-done | bytes 65568 | tf_op jit(solution)/shard_map/ppermute | solution.py:185
  24.0 7.5 %all-to-all-done.pieces = f32[16,80,256]{2,1,0:T(8,128)S(1)} async-done(((f32[16,80,256]{2,1,0:T(8,128)}), f32[16,80,256]{2,1,0:T(8,128)S(1)}, u32[]{:S(2)}, u32[]{:S(2)}) %all-to-all-start) | async-done | bytes 1310752 | tf_op jit(solution)/shard_map/all_to_all | solution.py:193
  31.5 0.7 %collective-permute-start.3 = (f32[80,128]{1,0:T(8,128)S(1)}, f32[80,128]{1,0:T(8,128)S(1)}, u32[]{:S(2)}, u32[]{:S(2)}) collective-permute-start(f32[80,128]{1,0:T(8,128)S(1)} %slice_bitcast_fusion), channel_id=1, source_target_pairs={{0,16},{1,17},{2,18},{3,19},{4,20},{5,21},{6,22},{7,23},{8,24},{9,... | collective-permute-start | bytes 122888 | tf_op jit(solution)/shard_map/ppermute | solution.py:185
  32.2 0.0 collective-permute-done.3
  32.2 0.7 %collective-permute-start.4 = (f32[80,128]{1,0:T(8,128)S(1)}, f32[80,128]{1,0:T(8,128)S(1)}, u32[]{:S(2)}, u32[]{:S(2)}) collective-permute-start(f32[80,128]{1,0:T(8,128)S(1)} %broadcast_select_fusion.3), channel_id=1, source_target_pairs={{0,32},{16,48},{1,33},{17,49},{2,34},{18,50},{3,35},{19,51},{4,36}... | collective-permute-start | bytes 122888 | tf_op jit(solution)/shard_map/ppermute | solution.py:185
  32.9 0.0 collective-permute-done.4
  32.9 1.3 %collective-permute-start.5 = (f32[80,128]{1,0:T(8,128)S(1)}, f32[80,128]{1,0:T(8,128)S(1)}, u32[]{:S(2)}, u32[]{:S(2)}) collective-permute-start(f32[80,128]{1,0:T(8,128)S(1)} %broadcast_select_fusion.4.kept_ref), channel_id=1, source_target_pairs={{0,64},{16,80},{32,96},{48,112},{1,65},{17,81},{33,97},{49,113},{2... | collective-permute-start | bytes 122888 | tf_op jit(solution)/shard_map/ppermute | solution.py:185
  34.2 0.1 add_convert_fusion.place_ref
  34.3 8.3 %collective-permute-done.5.arrived_ref = f32[80,128]{1,0:T(8,128)S(1)} collective-permute-done((f32[80,128]{1,0:T(8,128)S(1)}, f32[80,128]{1,0:T(8,128)S(1)}, u32[]{:S(2)}, u32[]{:S(2)}) %collective-permute-start.5) | collective-permute-done | bytes 40992 | tf_op jit(solution)/shard_map/ppermute | solution.py:185
  42.6 0.0 copy-done
  42.6 6.3 %factor_and_update.1 = (f32[4096,256]{1,0:T(8,128)}, f32[16,4096]{1,0:T(8,128)}, f32[64,256]{1,0:T(8,128)}) custom-call(s32[2]{0:T(128)S(1)} %add_convert_fusion.place_ref, f32[16,80,256]{2,1,0:T(8,128)S(1)} %all-to-all-done.pieces, f32[80,128]{1,0:T(8,128)S(1)} %broadcast_select_fusion.4.kept_ref, f32[80,128]{1,0:T(8,128)S(1)} %collective-permute-done.5.arrived_ref, ...), custom_call_target="tpu_custom_call" | custom-call | flops 402653184 | bytes 8388608 | tf_op jit(solution)/shard_map/factor_and_update/pallas_call | solution.py:154
  (5 shorter events, 0.0 us)
Async XLA Ops:
  0.6 42.0 %copy-start = (f32[64,256]{1,0:T(8,128)S(1)}, f32[64,256]{1,0:T(8,128)}, u32[]{:S(2)}) copy-start(f32[64,256]{1,0:T(8,128)} %panel_ref.3) | copy-start | bytes 196612
  2.8 28.7 %all-to-all-start = ((f32[16,80,256]{2,1,0:T(8,128)}), f32[16,80,256]{2,1,0:T(8,128)S(1)}, u32[]{:S(2)}, u32[]{:S(2)}) async-start(f32[16,80,256]{2,1,0:T(8,128)} %pack_pieces.1), calls=%async_computation | async-start | bytes 2621440 | tf_op jit(solution)/shard_map/all_to_all | solution.py:193
  11.5 0.7 %collective-permute-start = (f32[64,256]{1,0:T(8,128)S(1)}, f32[64,256]{1,0:T(8,128)S(1)}, u32[]{:S(2)}, u32[]{:S(2)}) collective-permute-start(f32[64,256]{1,0:T(8,128)S(1)} %slice.7), channel_id=1, source_target_pairs={{0,16},{1,17},{2,18},{3,19},{4,20},{5,21},{6,22},{7,23},{8,24},{9,... | collective-permute-start | bytes 196616 | tf_op jit(solution)/shard_map/ppermute | solution.py:185
  13.1 0.7 %collective-permute-start.1 = (f32[64,256]{1,0:T(8,128)S(1)}, f32[64,256]{1,0:T(8,128)S(1)}, u32[]{:S(2)}, u32[]{:S(2)}) collective-permute-start(f32[64,256]{1,0:T(8,128)S(1)} %broadcast_select_fusion), channel_id=1, source_target_pairs={{0,32},{16,48},{1,33},{17,49},{2,34},{18,50},{3,35},{19,51},{4,36}... | collective-permute-start | bytes 196616 | tf_op jit(solution)/shard_map/ppermute | solution.py:185
  13.8 10.2 %collective-permute-start.2 = (f32[64,256]{1,0:T(8,128)S(1)}, f32[64,256]{1,0:T(8,128)S(1)}, u32[]{:S(2)}, u32[]{:S(2)}) collective-permute-start(f32[64,256]{1,0:T(8,128)S(1)} %broadcast_select_fusion.1), channel_id=1, source_target_pairs={{0,64},{16,80},{32,96},{48,112},{1,65},{17,81},{33,97},{49,113},{2... | collective-permute-start | bytes 196616 | tf_op jit(solution)/shard_map/ppermute | solution.py:185
  31.5 0.7 %collective-permute-start.3 = (f32[80,128]{1,0:T(8,128)S(1)}, f32[80,128]{1,0:T(8,128)S(1)}, u32[]{:S(2)}, u32[]{:S(2)}) collective-permute-start(f32[80,128]{1,0:T(8,128)S(1)} %slice_bitcast_fusion), channel_id=1, source_target_pairs={{0,16},{1,17},{2,18},{3,19},{4,20},{5,21},{6,22},{7,23},{8,24},{9,... | collective-permute-start | bytes 122888 | tf_op jit(solution)/shard_map/ppermute | solution.py:185
  32.2 0.7 %collective-permute-start.4 = (f32[80,128]{1,0:T(8,128)S(1)}, f32[80,128]{1,0:T(8,128)S(1)}, u32[]{:S(2)}, u32[]{:S(2)}) collective-permute-start(f32[80,128]{1,0:T(8,128)S(1)} %broadcast_select_fusion.3), channel_id=1, source_target_pairs={{0,32},{16,48},{1,33},{17,49},{2,34},{18,50},{3,35},{19,51},{4,36}... | collective-permute-start | bytes 122888 | tf_op jit(solution)/shard_map/ppermute | solution.py:185
  32.9 9.7 %collective-permute-start.5 = (f32[80,128]{1,0:T(8,128)S(1)}, f32[80,128]{1,0:T(8,128)S(1)}, u32[]{:S(2)}, u32[]{:S(2)}) collective-permute-start(f32[80,128]{1,0:T(8,128)S(1)} %broadcast_select_fusion.4.kept_ref), channel_id=1, source_target_pairs={{0,64},{16,80},{32,96},{48,112},{1,65},{17,81},{33,97},{49,113},{2... | collective-permute-start | bytes 122888 | tf_op jit(solution)/shard_map/ppermute | solution.py:185

commit v5 on v4

--- a/solution.py
+++ b/solution.py
@@ -63,29 +63,32 @@
     return jnp.concatenate([block[:, width:] for block in blocks], 0)
 
 
-def pack_kernel(panel_ref, targets_ref, sent_ref):
+def pack_kernel(panel_ref, targets_ref, *sent_refs):
     width = panel_ref.shape[0]
-    for p in range(sent_ref.shape[0]):
-        sent_ref[p, :width, :] = panel_ref[...]
-        sent_ref[p, width:, :] = targets_ref[p]
+    for part, ref in enumerate(sent_refs):
+        lanes = slice(part * LANES, (part + 1) * LANES)
+        for p in range(ref.shape[0]):
+            ref[p, :width, :] = panel_ref[:, lanes]
+            ref[p, width:, :] = targets_ref[p, :, lanes]
 
 
 def pack(panel, targets):
     count, mine, wide = targets.shape
+    parts = wide // LANES
     vmem = pl.BlockSpec(memory_space=pltpu.VMEM)
     return pl.pallas_call(
         pack_kernel,
-        out_shape=jax.ShapeDtypeStruct((count, panel.shape[0] + mine, wide), jnp.float32),
+        out_shape=[jax.ShapeDtypeStruct((count, panel.shape[0] + mine, LANES), jnp.float32)] * parts,
         in_specs=[vmem, vmem],
-        out_specs=vmem,
+        out_specs=[vmem] * parts,
         name="pack_pieces",
     )(panel, targets)
 
 
-def step_kernel(place_ref, pieces, kept_ref, arrived_ref, slab_panel_ref, panel_ref, slab_ref,
+def step_kernel(place_ref, one_ref, two_ref, lead0_ref, lead1_ref, lead2_ref, lead3_ref, slab_ref,
                 slab_out, targets_out, factor_out, held, stacks, solved_targets, own_factor, arrive, leave, end):
-    count, _, wide = pieces.shape
-    width = panel_ref.shape[0]
+    count, depth, _ = one_ref.shape
+    width, wide = own_factor.shape
     each = count // GROUPS
     loads, stores = [], []
     for g in range(GROUPS):
@@ -97,16 +100,19 @@
     for load in loads:
         load.start()
     is_first = place_ref[0] == 1
-    lead_rows = jnp.where(place_ref[1] == 1, arrived_ref[...], kept_ref[...])
+    lead_rows = lead0_ref[...]
+    for number, ref in enumerate((lead1_ref, lead2_ref, lead3_ref)):
+        lead_rows = jnp.where(place_ref[1] == number + 1, ref[...], lead_rows)
     inverse = inverse_factor(lead_rows[:width], width)
-    slab_factor = exact(inverse, slab_panel_ref[...])
+    slab_panel = jnp.concatenate([lead_rows[i : i + width] for i in range(depth, lead_rows.shape[0], width)], 1)
+    slab_factor = exact(inverse, slab_panel)
     high, low = halves(slab_factor)
     slab_stack = jnp.concatenate([high, low, high], 0)
     high, middle, low = thirds(inverse)
     large = jnp.concatenate([high, high, middle, middle], 1)
     small = jnp.concatenate([high, low], 1)
     for p in range(count):
-        one, two, three = thirds(pieces[p, :width, :])
+        one, two, three = thirds(jnp.concatenate([one_ref[p, :width, :], two_ref[p, :width, :]], 1))
         solved = dot(large, jnp.concatenate([one, two, one, two], 0))
         solved = solved + dot(small, jnp.concatenate([three, one], 0))
         high, low = halves(solved)
@@ -123,14 +129,14 @@
                 held[:width, :] = slab_factor
 
         stores[g].start()
-    own_factor[...] = exact(inverse, panel_ref[...])
+    own_factor[...] = exact(inverse, jnp.concatenate([one_ref[place_ref[2], :width, :], two_ref[place_ref[2], :width, :]], 1))
     stores[GROUPS].start()
-    lead = exact(lead_rows[width:, :width], inverse, ((1,), (1,)))
+    lead = exact(lead_rows[width:depth, :width], inverse, ((1,), (1,)))
     high, low = halves(lead)
     lead_stack = jnp.concatenate([high, low, high], 1)
     for p in range(count):
         product = dot(lead_stack, stacks[:, p * wide : (p + 1) * wide])
-        solved_targets[:, p * wide : (p + 1) * wide] = pieces[p, width:, :] - product
+        solved_targets[:, p * wide : (p + 1) * wide] = jnp.concatenate([one_ref[p, width:, :], two_ref[p, width:, :]], 1) - product
 
     @pl.when(is_first)
     def _():
@@ -141,26 +147,26 @@
         store.wait()
 
 
-def step(place, got, kept, arrived, slab_panel, panel, slab):
-    count, depth, wide = got.shape
-    width = panel.shape[0]
+def step(place, one, two, leads, width, slab):
+    count, depth, _ = one.shape
+    wide = slab.shape[1]
     vmem = pl.BlockSpec(memory_space=pltpu.VMEM)
     hbm = pl.BlockSpec(memory_space=pl.ANY)
     outputs = (
         jax.ShapeDtypeStruct(slab.shape, jnp.float32),
         jax.ShapeDtypeStruct((depth - width, count * wide), jnp.float32),
-        jax.ShapeDtypeStruct(panel.shape, jnp.float32),
+        jax.ShapeDtypeStruct((width, wide), jnp.float32),
     )
     return pl.pallas_call(
         step_kernel,
         out_shape=outputs,
-        in_specs=[pl.BlockSpec(memory_space=pltpu.SMEM), vmem, vmem, vmem, vmem, vmem, hbm],
+        in_specs=[pl.BlockSpec(memory_space=pltpu.SMEM), vmem, vmem, *[vmem] * len(leads), hbm],
         out_specs=(hbm, hbm, hbm),
         scratch_shapes=[
             pltpu.VMEM(slab.shape, jnp.float32),
             pltpu.VMEM((3 * width, count * wide), jnp.bfloat16),
             pltpu.VMEM(outputs[1].shape, jnp.float32),
-            pltpu.VMEM(panel.shape, jnp.float32),
+            pltpu.VMEM(outputs[2].shape, jnp.float32),
             pltpu.SemaphoreType.DMA((GROUPS,)),
             pltpu.SemaphoreType.DMA((GROUPS,)),
             pltpu.SemaphoreType.DMA((2,)),
@@ -170,33 +176,30 @@
             flops=6 * slab.size * width, bytes_accessed=8 * slab.size, transcendentals=width
         ),
         name="factor_and_update",
-    )(place, got, kept, arrived, slab_panel, panel, slab)
+    )(place, one, two, *leads, slab)
 
 
 def body(kernel_panel, kernel_slab, targets):
     width, wide = kernel_panel.shape
-    rows, cols = lax.axis_size("row"), lax.axis_size("col")
+    cols = lax.axis_size("col")
     row_index = lax.axis_index("row")
     mine = targets.shape[0] // cols
 
-    def down(value):
-        reach = 1
-        while True:
-            arrived = lax.ppermute(value, "row", [(i, i + reach) for i in range(reach)])
-            new = (row_index >= reach) & (row_index < 2 * reach)
-            reach = 2 * reach
-            if reach == rows:
-                return value, arrived, new
-            value = jnp.where(new, arrived, value)
-
-    sent = pack(kernel_panel, targets.reshape(cols, mine, wide))
-    got = lax.all_to_all(sent, "col", split_axis=0, concat_axis=0)
-    kept, arrived, new = down(kernel_slab[:width])
-    slab_panel = jnp.where(new, arrived, kept)
-    lead, slab_panel = lax.optimization_barrier((got[0, :, :LANES], slab_panel))
-    kept, arrived, new = down(lead)
-    place = jnp.stack([row_index == 0, new]).astype(jnp.int32)
-    return tuple(step(place, got, kept, arrived, slab_panel, kernel_panel, kernel_slab))
+    first, second = pack(kernel_panel, targets.reshape(cols, mine, wide))
+    first, slab = lax.optimization_barrier((first, kernel_slab))
+    one = lax.all_to_all(first, "col", split_axis=0, concat_axis=0)
+    two = lax.all_to_all(second, "col", split_axis=0, concat_axis=0)
+    head = jnp.concatenate([slab[:width, at : at + LANES] for at in range(0, wide, LANES)], 0)
+    one, head = lax.optimization_barrier((one, head))
+    lead = jnp.concatenate([one[0], head], 0)
+    arrived = lax.ppermute(lead, "row", [(0, 1)])
+    leads = [jnp.where(row_index == 1, arrived, lead)]
+    which = jnp.zeros_like(row_index)
+    for i in (4, 2, 6):
+        which = jnp.where(row_index // 2 * 2 == i, len(leads), which)
+        leads.append(lax.ppermute(leads[0], "row", [(0, i), (1, i + 1)]))
+    place = jnp.stack([(row_index == 0).astype(jnp.int32), which, lax.axis_index("col")])
+    return tuple(step(place, one, two, leads, width, kernel_slab))
 
 
 def solution(mesh):

time: 49.3 us -> 46.3 us (0.939)
  waiting for transfers between devices: 24.7 us -> 20.8 us
  starting transfers between devices: 13.1 us -> 14.8 us
  other arithmetic: 0.97 us -> 0.11 us
    ppermute x6 -> x4, waiting for transfers between devices: 17.2 us -> 0.01 us  [the longest x3 0.01 us: body(): leads.append(lax.ppermute(leads[0], 'row', [(0, i), (1, i + 1)]))]
    all_to_all x1 -> x2, waiting for transfers between devices: 7.5 us -> 20.8 us  [the longest x1 12.1 us: body(): one = lax.all_to_all(first, 'col', split_axis=0, concat_axis=0)]
    all_to_all x1 -> x2, starting transfers between devices: 7.88 us -> 11.5 us  [the longest x1 7.88 us: body(): one = lax.all_to_all(first, 'col', split_axis=0, concat_axis=0)]
    ppermute x6 -> x4, starting transfers between devices: 5.21 us -> 3.29 us  [the longest x3 2.63 us: body(): leads.append(lax.ppermute(leads[0], 'row', [(0, i), (1, i + 1)]))]
    select_n x5 -> x1, other arithmetic: 0.89 us -> 0.02 us  [body(): leads = [jnp.where(row_index == 1, arrived, lead)]]
  transfers between devices with their start and end apart: 7 -> 6, of which waited for: 3 -> 2; matrix products, arithmetic and copies ran while one was open for 4% -> 2% of each run, Pallas kernels for 0% -> 0%
where the time goes in v5:
time: 46.3 us; the launch traced here: 45.8 us
  waiting for transfers between devices  20.8 us (45%)
  starting transfers between devices  14.8 us (32%)
  Pallas kernels  8.54 us (18%)
  local copies, waits for them, and re-layouts  0.79 us (2%)
  between operations  0.75 us (2%)
    all_to_all x1, waiting for transfers between devices, body(): one = lax.all_to_all(first, 'col', split_axis=0, concat_axis=0)  12.1 us
    all_to_all x1, waiting for transfers between devices, body(): two = lax.all_to_all(second, 'col', split_axis=0, concat_axis=0)  8.65 us
    all_to_all x1, starting transfers between devices, body(): one = lax.all_to_all(first, 'col', split_axis=0, concat_axis=0)  7.88 us
    pallas_call x1, Pallas kernels, step(): pl.pallas_call(step_kernel, out_shape=outputs, in_specs=[pl.BlockSpec(mem...  6.46 us
    all_to_all x1, starting transfers between devices, body(): two = lax.all_to_all(second, 'col', split_axis=0, concat_axis=0)  3.59 us
    ppermute x3, starting transfers between devices, body(): leads.append(lax.ppermute(leads[0], 'row', [(0, i), (1, i + 1)]))  2.63 us
    pallas_call x1, Pallas kernels, pack(): pl.pallas_call(pack_kernel, out_shape=[jax.ShapeDtypeStruct((count, panel...  2.08 us
  transfers between devices with their start and end apart: 6, of which 2 were waited for; matrix products, arithmetic and copies ran while one was open for 2% of the time, Pallas kernels for 0%

profile of v5, /device:TPU:24, one launch (start us, length us, event | category | flops | bytes accessed | tf_op | source)
XLA Modules:
  0.0 45.8 jit_solution(15649642060684627005)
XLA Ops:
  0.6 2.1 %pack_pieces.1 = (f32[16,80,128]{2,1,0:T(8,128)}, f32[16,80,128]{2,1,0:T(8,128)}) custom-call(f32[64,256]{1,0:T(8,128)} %panel_ref.1, f32[16,16,256]{2,1,0:T(8,128)} %bitcast.6), custom_call_target="tpu_custom_call" | custom-call | tf_op jit(solution)/shard_map/pack_pieces/pallas_call | solution.py:79
  2.7 7.9 %all-to-all-start = ((f32[16,80,128]{2,1,0:T(8,128)}), f32[16,80,128]{2,1,0:T(8,128)S(1)}, u32[]{:S(2)}, u32[]{:S(2)}) async-start(f32[16,80,128]{2,1,0:T(8,128)} %get-tuple-element.10), calls=%async_computation | async-start | bytes 1310720 | tf_op jit(solution)/shard_map/all_to_all | solution.py:190
  10.6 0.8 %fusion = (f32[64,128]{1,0:T(8,128)S(1)}, f32[64,128]{1,0:T(8,128)S(1)}) fusion(f32[4096,256]{1,0:T(8,128)} %slab_ref.1), kind=kLoop, calls=%fused_computation.5 | loop fusion | bytes 131072 | tf_op jit(solution)/shard_map/slice | solution.py:192
  11.4 12.1 %all-to-all-done.one_ref = f32[16,80,128]{2,1,0:T(8,128)S(1)} async-done(((f32[16,80,128]{2,1,0:T(8,128)}), f32[16,80,128]{2,1,0:T(8,128)S(1)}, u32[]{:S(2)}, u32[]{:S(2)}) %all-to-all-start) | async-done | bytes 655392 | tf_op jit(solution)/shard_map/all_to_all | solution.py:190
  23.5 3.6 %all-to-all-start.1 = ((f32[16,80,128]{2,1,0:T(8,128)}), f32[16,80,128]{2,1,0:T(8,128)S(1)}, u32[]{:S(2)}, u32[]{:S(2)}) async-start(f32[16,80,128]{2,1,0:T(8,128)} %get-tuple-element.13), calls=%async_computation.1 | async-start | bytes 1310720 | tf_op jit(solution)/shard_map/all_to_all | solution.py:191
  27.2 0.7 %collective-permute-start = (f32[208,128]{1,0:T(8,128)S(1)}, f32[208,128]{1,0:T(8,128)S(1)}, u32[]{:S(2)}, u32[]{:S(2)}) collective-permute-start(f32[208,128]{1,0:T(8,128)S(1)} %pad_maximum_fusion), channel_id=1, source_target_pairs={{0,16},{1,17},{2,18},{3,19},{4,20},{5,21},{6,22},{7,23},{8,24},{9,... | collective-permute-start | bytes 319496 | tf_op jit(solution)/shard_map/ppermute | solution.py:195
  27.9 0.0 collective-permute-done
  27.9 1.3 %collective-permute-start.3 = (f32[208,128]{1,0:T(8,128)S(1)}, f32[208,128]{1,0:T(8,128)S(1)}, u32[]{:S(2)}, u32[]{:S(2)}) collective-permute-start(f32[208,128]{1,0:T(8,128)S(1)} %broadcast_select_fusion.lead0_ref), channel_id=1, source_target_pairs={{0,96},{16,112},{1,97},{17,113},{2,98},{18,114},{3,99},{19,115},{4... | collective-permute-start | bytes 319496 | tf_op jit(solution)/shard_map/ppermute | solution.py:200
  29.2 0.7 %collective-permute-start.2 = (f32[208,128]{1,0:T(8,128)S(1)}, f32[208,128]{1,0:T(8,128)S(1)}, u32[]{:S(2)}, u32[]{:S(2)}) collective-permute-start(f32[208,128]{1,0:T(8,128)S(1)} %broadcast_select_fusion.lead0_ref), channel_id=1, source_target_pairs={{0,32},{16,48},{1,33},{17,49},{2,34},{18,50},{3,35},{19,51},{4,36}... | collective-permute-start | bytes 319496 | tf_op jit(solution)/shard_map/ppermute | solution.py:200
  29.9 0.7 %collective-permute-start.1 = (f32[208,128]{1,0:T(8,128)S(1)}, f32[208,128]{1,0:T(8,128)S(1)}, u32[]{:S(2)}, u32[]{:S(2)}) collective-permute-start(f32[208,128]{1,0:T(8,128)S(1)} %broadcast_select_fusion.lead0_ref), channel_id=1, source_target_pairs={{0,64},{16,80},{1,65},{17,81},{2,66},{18,82},{3,67},{19,83},{4,68}... | collective-permute-start | bytes 319496 | tf_op jit(solution)/shard_map/ppermute | solution.py:200
  30.6 0.1 pad_add_fusion.place_ref
  30.6 8.6 %all-to-all-done.1.two_ref = f32[16,80,128]{2,1,0:T(8,128)S(1)} async-done(((f32[16,80,128]{2,1,0:T(8,128)}), f32[16,80,128]{2,1,0:T(8,128)S(1)}, u32[]{:S(2)}, u32[]{:S(2)}) %all-to-all-start.1) | async-done | bytes 655392 | tf_op jit(solution)/shard_map/all_to_all | solution.py:191
  39.3 0.0 collective-permute-done.3.lead3_ref
  39.3 0.0 collective-permute-done.2.lead2_ref
  39.3 0.0 collective-permute-done.1.lead1_ref
  39.3 6.5 %factor_and_update.1 = (f32[4096,256]{1,0:T(8,128)}, f32[16,4096]{1,0:T(8,128)}, f32[64,256]{1,0:T(8,128)}) custom-call(s32[3]{0:T(128)S(1)} %pad_add_fusion.place_ref, f32[16,80,128]{2,1,0:T(8,128)S(1)} %all-to-all-done.one_ref, f32[16,80,128]{2,1,0:T(8,128)S(1)} %all-to-all-done.1.two_ref, f32[208,128]{1,0:T(8,128)S(1)} %broadcast_select_fusion.lead0_ref, ...), custom_call_target="tpu_custom_call" | custom-call | flops 402653184 | bytes 8388608 | tf_op jit(solution)/shard_map/factor_and_update/pallas_call | solution.py:160
  (4 shorter events, 0.0 us)
Async XLA Ops:
  2.7 20.8 %all-to-all-start = ((f32[16,80,128]{2,1,0:T(8,128)}), f32[16,80,128]{2,1,0:T(8,128)S(1)}, u32[]{:S(2)}, u32[]{:S(2)}) async-start(f32[16,80,128]{2,1,0:T(8,128)} %get-tuple-element.10), calls=%async_computation | async-start | bytes 1310720 | tf_op jit(solution)/shard_map/all_to_all | solution.py:190
  23.5 15.7 %all-to-all-start.1 = ((f32[16,80,128]{2,1,0:T(8,128)}), f32[16,80,128]{2,1,0:T(8,128)S(1)}, u32[]{:S(2)}, u32[]{:S(2)}) async-start(f32[16,80,128]{2,1,0:T(8,128)} %get-tuple-element.13), calls=%async_computation.1 | async-start | bytes 1310720 | tf_op jit(solution)/shard_map/all_to_all | solution.py:191
  27.2 0.7 %collective-permute-start = (f32[208,128]{1,0:T(8,128)S(1)}, f32[208,128]{1,0:T(8,128)S(1)}, u32[]{:S(2)}, u32[]{:S(2)}) collective-permute-start(f32[208,128]{1,0:T(8,128)S(1)} %pad_maximum_fusion), channel_id=1, source_target_pairs={{0,16},{1,17},{2,18},{3,19},{4,20},{5,21},{6,22},{7,23},{8,24},{9,... | collective-permute-start | bytes 319496 | tf_op jit(solution)/shard_map/ppermute | solution.py:195
  27.9 11.4 %collective-permute-start.3 = (f32[208,128]{1,0:T(8,128)S(1)}, f32[208,128]{1,0:T(8,128)S(1)}, u32[]{:S(2)}, u32[]{:S(2)}) collective-permute-start(f32[208,128]{1,0:T(8,128)S(1)} %broadcast_select_fusion.lead0_ref), channel_id=1, source_target_pairs={{0,96},{16,112},{1,97},{17,113},{2,98},{18,114},{3,99},{19,115},{4... | collective-permute-start | bytes 319496 | tf_op jit(solution)/shard_map/ppermute | solution.py:200
  29.2 10.1 %collective-permute-start.2 = (f32[208,128]{1,0:T(8,128)S(1)}, f32[208,128]{1,0:T(8,128)S(1)}, u32[]{:S(2)}, u32[]{:S(2)}) collective-permute-start(f32[208,128]{1,0:T(8,128)S(1)} %broadcast_select_fusion.lead0_ref), channel_id=1, source_target_pairs={{0,32},{16,48},{1,33},{17,49},{2,34},{18,50},{3,35},{19,51},{4,36}... | collective-permute-start | bytes 319496 | tf_op jit(solution)/shard_map/ppermute | solution.py:200
  29.9 9.4 %collective-permute-start.1 = (f32[208,128]{1,0:T(8,128)S(1)}, f32[208,128]{1,0:T(8,128)S(1)}, u32[]{:S(2)}, u32[]{:S(2)}) collective-permute-start(f32[208,128]{1,0:T(8,128)S(1)} %broadcast_select_fusion.lead0_ref), channel_id=1, source_target_pairs={{0,64},{16,80},{1,65},{17,81},{2,66},{18,82},{3,67},{19,83},{4,68}... | collective-permute-start | bytes 319496 | tf_op jit(solution)/shard_map/ppermute | solution.py:200

commit v6 on v5

--- a/solution.py
+++ b/solution.py
@@ -49,7 +49,6 @@
         for j in range(SUB):
             pivot = jnp.broadcast_to(spread[j][b][j : j + 1, :], shape)
             scale = lax.rsqrt(pivot)
-            scale = scale * (1.5 - 0.5 * (pivot * scale) * scale)
             top = jnp.broadcast_to(blocks[b][j : j + 1, :], shape) * scale
             factor = {i: spread[j][i] * scale for i in below}
             factor[b] = jnp.where(row > j, spread[j][b] * scale, 0.0)
@@ -63,24 +62,26 @@
     return jnp.concatenate([block[:, width:] for block in blocks], 0)
 
 
-def pack_kernel(panel_ref, targets_ref, *sent_refs):
+def pack_kernel(panel_ref, targets_ref, sent_ref):
     width = panel_ref.shape[0]
-    for part, ref in enumerate(sent_refs):
-        lanes = slice(part * LANES, (part + 1) * LANES)
-        for p in range(ref.shape[0]):
-            ref[p, :width, :] = panel_ref[:, lanes]
-            ref[p, width:, :] = targets_ref[p, :, lanes]
-
-
-def pack(panel, targets):
-    count, mine, wide = targets.shape
-    parts = wide // LANES
-    vmem = pl.BlockSpec(memory_space=pltpu.VMEM)
+    for p in range(sent_ref.shape[0]):
+        sent_ref[p, :width, :] = panel_ref[...]
+        sent_ref[p, width:, :] = targets_ref[p]
+
+
+def pack(panel, targets, part):
+    count, mine, _ = targets.shape
+    width = panel.shape[0]
+    sent = (count, width + mine, LANES)
     return pl.pallas_call(
         pack_kernel,
-        out_shape=[jax.ShapeDtypeStruct((count, panel.shape[0] + mine, LANES), jnp.float32)] * parts,
-        in_specs=[vmem, vmem],
-        out_specs=[vmem] * parts,
+        grid=(1,),
+        out_shape=jax.ShapeDtypeStruct(sent, jnp.float32),
+        in_specs=[
+            pl.BlockSpec((width, LANES), lambda i: (0, part)),
+            pl.BlockSpec((count, mine, LANES), lambda i: (0, 0, part)),
+        ],
+        out_specs=pl.BlockSpec(sent, lambda i: (0, 0, 0)),
         name="pack_pieces",
     )(panel, targets)
 
@@ -185,12 +186,14 @@
     row_index = lax.axis_index("row")
     mine = targets.shape[0] // cols
 
-    first, second = pack(kernel_panel, targets.reshape(cols, mine, wide))
-    first, slab = lax.optimization_barrier((first, kernel_slab))
+    target_rows = targets.reshape(cols, mine, wide)
+    first = pack(kernel_panel, target_rows, 0)
+    first, panel, target_rows, slab = lax.optimization_barrier((first, kernel_panel, target_rows, kernel_slab))
+    second = pack(panel, target_rows, 1)
     one = lax.all_to_all(first, "col", split_axis=0, concat_axis=0)
+    head = jnp.concatenate([slab[:width, at : at + LANES] for at in range(0, wide, LANES)], 0)
+    one, head, second = lax.optimization_barrier((one, head, second))
     two = lax.all_to_all(second, "col", split_axis=0, concat_axis=0)
-    head = jnp.concatenate([slab[:width, at : at + LANES] for at in range(0, wide, LANES)], 0)
-    one, head = lax.optimization_barrier((one, head))
     lead = jnp.concatenate([one[0], head], 0)
     arrived = lax.ppermute(lead, "row", [(0, 1)])
     leads = [jnp.where(row_index == 1, arrived, lead)]

time: 46.3 us -> 45.6 us (0.985)
  waiting for transfers between devices: 20.8 us -> 19 us
  Pallas kernels: 8.54 us -> 9.59 us
    all_to_all x1, waiting for transfers between devices: 8.65 us -> 3.56 us  [body(): two = lax.all_to_all(second, 'col', split_axis=0, concat_axis=0)]
    ppermute x3, waiting for transfers between devices: 0.01 us -> 5.08 us  [body(): leads.append(lax.ppermute(leads[0], 'row', [(0, i), (1, i + 1)]))]
    all_to_all x1, waiting for transfers between devices: 12.1 us -> 10.3 us  [body(): one = lax.all_to_all(first, 'col', split_axis=0, concat_axis=0)]
    pallas_call x1 -> x2, Pallas kernels: 2.08 us -> 3.61 us  [pack(): pl.pallas_call(pack_kernel, grid=(1,), out_shape=jax.ShapeDtypeStruct(sen...]
    pallas_call x1, Pallas kernels: 6.46 us -> 5.98 us  [step(): pl.pallas_call(step_kernel, out_shape=outputs, in_specs=[pl.BlockSpec(mem...]
  transfers between devices with their start and end apart: 6 -> 6, of which waited for: 2 -> 3; matrix products, arithmetic and copies ran while one was open for 2% -> 2% of each run, Pallas kernels for 0% -> 4%
where the time goes in v6:
time: 45.6 us; the launch traced here: 45 us
  waiting for transfers between devices  19 us (42%)
  starting transfers between devices  14.8 us (32%)
  Pallas kernels  9.59 us (21%)
  local copies, waits for them, and re-layouts  0.78 us (2%)
  between operations  0.74 us (2%)
    all_to_all x1, waiting for transfers between devices, body(): one = lax.all_to_all(first, 'col', split_axis=0, concat_axis=0)  10.3 us
    all_to_all x1, starting transfers between devices, body(): one = lax.all_to_all(first, 'col', split_axis=0, concat_axis=0)  7.88 us
    pallas_call x1, Pallas kernels, step(): pl.pallas_call(step_kernel, out_shape=outputs, in_specs=[pl.BlockSpec(mem...  5.98 us
    ppermute x3, waiting for transfers between devices, body(): leads.append(lax.ppermute(leads[0], 'row', [(0, i), (1, i + 1)]))  5.08 us
    pallas_call x2, Pallas kernels, pack(): pl.pallas_call(pack_kernel, grid=(1,), out_shape=jax.ShapeDtypeStruct(sen...  3.61 us
    all_to_all x1, starting transfers between devices, body(): two = lax.all_to_all(second, 'col', split_axis=0, concat_axis=0)  3.59 us
    all_to_all x1, waiting for transfers between devices, body(): two = lax.all_to_all(second, 'col', split_axis=0, concat_axis=0)  3.56 us
    ppermute x3, starting transfers between devices, body(): leads.append(lax.ppermute(leads[0], 'row', [(0, i), (1, i + 1)]))  2.63 us
  transfers between devices with their start and end apart: 6, of which 3 were waited for; matrix products, arithmetic and copies ran while one was open for 2% of the time, Pallas kernels for 4%

profile of v6, /device:TPU:24, one launch (start us, length us, event | category | flops | bytes accessed | tf_op | source)
XLA Modules:
  0.0 45.0 jit_solution(16376036314650279742)
XLA Ops:
  0.6 1.8 %pack_pieces.2 = f32[16,80,128]{2,1,0:T(8,128)} custom-call(f32[64,256]{1,0:T(8,128)} %panel_ref.2, f32[16,16,256]{2,1,0:T(8,128)} %bitcast.6), custom_call_target="tpu_custom_call" | custom-call | tf_op jit(solution)/shard_map/pack_pieces/pallas_call | solution.py:76
  2.4 7.9 %all-to-all-start = ((f32[16,80,128]{2,1,0:T(8,128)}), f32[16,80,128]{2,1,0:T(8,128)S(1)}, u32[]{:S(2)}, u32[]{:S(2)}) async-start(f32[16,80,128]{2,1,0:T(8,128)} %pack_pieces.2), calls=%async_computation | async-start | bytes 1310720 | tf_op jit(solution)/shard_map/all_to_all | solution.py:193
  10.3 1.8 %pack_pieces.3 = f32[16,80,128]{2,1,0:T(8,128)} custom-call(f32[64,256]{1,0:T(8,128)} %panel_ref.2, f32[16,16,256]{2,1,0:T(8,128)} %bitcast.7), custom_call_target="tpu_custom_call" | custom-call | tf_op jit(solution)/shard_map/pack_pieces/pallas_call | solution.py:76
  12.1 0.8 %fusion = (f32[64,128]{1,0:T(8,128)S(1)}, f32[64,128]{1,0:T(8,128)S(1)}) fusion(f32[4096,256]{1,0:T(8,128)} %slab_ref.1), kind=kLoop, calls=%fused_computation.5 | loop fusion | bytes 131072 | tf_op jit(solution)/shard_map/slice | solution.py:194
  12.9 10.3 %all-to-all-done.one_ref = f32[16,80,128]{2,1,0:T(8,128)S(1)} async-done(((f32[16,80,128]{2,1,0:T(8,128)}), f32[16,80,128]{2,1,0:T(8,128)S(1)}, u32[]{:S(2)}, u32[]{:S(2)}) %all-to-all-start) | async-done | bytes 655392 | tf_op jit(solution)/shard_map/all_to_all | solution.py:193
  23.3 3.6 %all-to-all-start.1 = ((f32[16,80,128]{2,1,0:T(8,128)}), f32[16,80,128]{2,1,0:T(8,128)S(1)}, u32[]{:S(2)}, u32[]{:S(2)}) async-start(f32[16,80,128]{2,1,0:T(8,128)} %pack_pieces.3), calls=%async_computation.1 | async-start | bytes 1310720 | tf_op jit(solution)/shard_map/all_to_all | solution.py:196
  26.9 0.7 %collective-permute-start = (f32[208,128]{1,0:T(8,128)S(1)}, f32[208,128]{1,0:T(8,128)S(1)}, u32[]{:S(2)}, u32[]{:S(2)}) collective-permute-start(f32[208,128]{1,0:T(8,128)S(1)} %pad_maximum_fusion), channel_id=1, source_target_pairs={{0,16},{1,17},{2,18},{3,19},{4,20},{5,21},{6,22},{7,23},{8,24},{9,... | collective-permute-start | bytes 319496 | tf_op jit(solution)/shard_map/ppermute | solution.py:198
  27.6 0.0 collective-permute-done
  27.6 1.3 %collective-permute-start.3 = (f32[208,128]{1,0:T(8,128)S(1)}, f32[208,128]{1,0:T(8,128)S(1)}, u32[]{:S(2)}, u32[]{:S(2)}) collective-permute-start(f32[208,128]{1,0:T(8,128)S(1)} %broadcast_select_fusion.lead0_ref), channel_id=1, source_target_pairs={{0,96},{16,112},{1,97},{17,113},{2,98},{18,114},{3,99},{19,115},{4... | collective-permute-start | bytes 319496 | tf_op jit(solution)/shard_map/ppermute | solution.py:203
  28.9 0.7 %collective-permute-start.2 = (f32[208,128]{1,0:T(8,128)S(1)}, f32[208,128]{1,0:T(8,128)S(1)}, u32[]{:S(2)}, u32[]{:S(2)}) collective-permute-start(f32[208,128]{1,0:T(8,128)S(1)} %broadcast_select_fusion.lead0_ref), channel_id=1, source_target_pairs={{0,32},{16,48},{1,33},{17,49},{2,34},{18,50},{3,35},{19,51},{4,36}... | collective-permute-start | bytes 319496 | tf_op jit(solution)/shard_map/ppermute | solution.py:203
  29.6 0.7 %collective-permute-start.1 = (f32[208,128]{1,0:T(8,128)S(1)}, f32[208,128]{1,0:T(8,128)S(1)}, u32[]{:S(2)}, u32[]{:S(2)}) collective-permute-start(f32[208,128]{1,0:T(8,128)S(1)} %broadcast_select_fusion.lead0_ref), channel_id=1, source_target_pairs={{0,64},{16,80},{1,65},{17,81},{2,66},{18,82},{3,67},{19,83},{4,68}... | collective-permute-start | bytes 319496 | tf_op jit(solution)/shard_map/ppermute | solution.py:203
  30.3 0.1 pad_add_fusion.place_ref
  30.4 5.1 %collective-permute-done.3.lead3_ref = f32[208,128]{1,0:T(8,128)S(1)} collective-permute-done((f32[208,128]{1,0:T(8,128)S(1)}, f32[208,128]{1,0:T(8,128)S(1)}, u32[]{:S(2)}, u32[]{:S(2)}) %collective-permute-start.3) | collective-permute-done | bytes 106528 | tf_op jit(solution)/shard_map/ppermute | solution.py:203
  35.4 0.0 collective-permute-done.2.lead2_ref
  35.4 0.0 collective-permute-done.1.lead1_ref
  35.4 3.6 %all-to-all-done.1.two_ref = f32[16,80,128]{2,1,0:T(8,128)S(1)} async-done(((f32[16,80,128]{2,1,0:T(8,128)}), f32[16,80,128]{2,1,0:T(8,128)S(1)}, u32[]{:S(2)}, u32[]{:S(2)}) %all-to-all-start.1) | async-done | bytes 655392 | tf_op jit(solution)/shard_map/all_to_all | solution.py:196
  39.0 6.0 %factor_and_update.1 = (f32[4096,256]{1,0:T(8,128)}, f32[16,4096]{1,0:T(8,128)}, f32[64,256]{1,0:T(8,128)}) custom-call(s32[3]{0:T(128)S(1)} %pad_add_fusion.place_ref, f32[16,80,128]{2,1,0:T(8,128)S(1)} %all-to-all-done.one_ref, f32[16,80,128]{2,1,0:T(8,128)S(1)} %all-to-all-done.1.two_ref, f32[208,128]{1,0:T(8,128)S(1)} %broadcast_select_fusion.lead0_ref, ...), custom_call_target="tpu_custom_call" | custom-call | flops 402653184 | bytes 8388608 | tf_op jit(solution)/shard_map/factor_and_update/pallas_call | solution.py:161
  (4 shorter events, 0.0 us)
Async XLA Ops:
  2.4 20.8 %all-to-all-start = ((f32[16,80,128]{2,1,0:T(8,128)}), f32[16,80,128]{2,1,0:T(8,128)S(1)}, u32[]{:S(2)}, u32[]{:S(2)}) async-start(f32[16,80,128]{2,1,0:T(8,128)} %pack_pieces.2), calls=%async_computation | async-start | bytes 1310720 | tf_op jit(solution)/shard_map/all_to_all | solution.py:193
  23.3 15.7 %all-to-all-start.1 = ((f32[16,80,128]{2,1,0:T(8,128)}), f32[16,80,128]{2,1,0:T(8,128)S(1)}, u32[]{:S(2)}, u32[]{:S(2)}) async-start(f32[16,80,128]{2,1,0:T(8,128)} %pack_pieces.3), calls=%async_computation.1 | async-start | bytes 1310720 | tf_op jit(solution)/shard_map/all_to_all | solution.py:196
  26.9 0.7 %collective-permute-start = (f32[208,128]{1,0:T(8,128)S(1)}, f32[208,128]{1,0:T(8,128)S(1)}, u32[]{:S(2)}, u32[]{:S(2)}) collective-permute-start(f32[208,128]{1,0:T(8,128)S(1)} %pad_maximum_fusion), channel_id=1, source_target_pairs={{0,16},{1,17},{2,18},{3,19},{4,20},{5,21},{6,22},{7,23},{8,24},{9,... | collective-permute-start | bytes 319496 | tf_op jit(solution)/shard_map/ppermute | solution.py:198
  27.6 7.8 %collective-permute-start.3 = (f32[208,128]{1,0:T(8,128)S(1)}, f32[208,128]{1,0:T(8,128)S(1)}, u32[]{:S(2)}, u32[]{:S(2)}) collective-permute-start(f32[208,128]{1,0:T(8,128)S(1)} %broadcast_select_fusion.lead0_ref), channel_id=1, source_target_pairs={{0,96},{16,112},{1,97},{17,113},{2,98},{18,114},{3,99},{19,115},{4... | collective-permute-start | bytes 319496 | tf_op jit(solution)/shard_map/ppermute | solution.py:203
  28.9 6.5 %collective-permute-start.2 = (f32[208,128]{1,0:T(8,128)S(1)}, f32[208,128]{1,0:T(8,128)S(1)}, u32[]{:S(2)}, u32[]{:S(2)}) collective-permute-start(f32[208,128]{1,0:T(8,128)S(1)} %broadcast_select_fusion.lead0_ref), channel_id=1, source_target_pairs={{0,32},{16,48},{1,33},{17,49},{2,34},{18,50},{3,35},{19,51},{4,36}... | collective-permute-start | bytes 319496 | tf_op jit(solution)/shard_map/ppermute | solution.py:203
  29.6 5.8 %collective-permute-start.1 = (f32[208,128]{1,0:T(8,128)S(1)}, f32[208,128]{1,0:T(8,128)S(1)}, u32[]{:S(2)}, u32[]{:S(2)}) collective-permute-start(f32[208,128]{1,0:T(8,128)S(1)} %broadcast_select_fusion.lead0_ref), channel_id=1, source_target_pairs={{0,64},{16,80},{1,65},{17,81},{2,66},{18,82},{3,67},{19,83},{4,68}... | collective-permute-start | bytes 319496 | tf_op jit(solution)/shard_map/ppermute | solution.py:203

commit v7 on v6

--- a/solution.py
+++ b/solution.py
@@ -87,7 +87,7 @@
 
 
 def step_kernel(place_ref, one_ref, two_ref, lead0_ref, lead1_ref, lead2_ref, lead3_ref, slab_ref,
-                slab_out, targets_out, factor_out, held, stacks, solved_targets, own_factor, arrive, leave, end):
+                slab_out, targets_out, factor_out, held, parts, stacks, solved_targets, own_factor, arrive, leave, end):
     count, depth, _ = one_ref.shape
     width, wide = own_factor.shape
     each = count // GROUPS
@@ -104,18 +104,21 @@
     lead_rows = lead0_ref[...]
     for number, ref in enumerate((lead1_ref, lead2_ref, lead3_ref)):
         lead_rows = jnp.where(place_ref[1] == number + 1, ref[...], lead_rows)
+    for p in range(count):
+        one, two, three = thirds(jnp.concatenate([one_ref[p, :width, :], two_ref[p, :width, :]], 1))
+        for i, part in enumerate((one, two, three, one)):
+            parts[i * width : (i + 1) * width, p * wide : (p + 1) * wide] = part
     inverse = inverse_factor(lead_rows[:width], width)
     slab_panel = jnp.concatenate([lead_rows[i : i + width] for i in range(depth, lead_rows.shape[0], width)], 1)
     slab_factor = exact(inverse, slab_panel)
     high, low = halves(slab_factor)
     slab_stack = jnp.concatenate([high, low, high], 0)
     high, middle, low = thirds(inverse)
-    large = jnp.concatenate([high, high, middle, middle], 1)
-    small = jnp.concatenate([high, low], 1)
+    large = jnp.concatenate([high, high, high, middle], 1)
+    small = jnp.concatenate([low, middle], 1)
     for p in range(count):
-        one, two, three = thirds(jnp.concatenate([one_ref[p, :width, :], two_ref[p, :width, :]], 1))
-        solved = dot(large, jnp.concatenate([one, two, one, two], 0))
-        solved = solved + dot(small, jnp.concatenate([three, one], 0))
+        piece = parts[:, p * wide : (p + 1) * wide]
+        solved = dot(large, piece) + dot(small, piece[: 2 * width])
         high, low = halves(solved)
         stacks[:, p * wide : (p + 1) * wide] = jnp.concatenate([high, high, low], 0)
     for g in range(GROUPS):
@@ -165,6 +168,7 @@
         out_specs=(hbm, hbm, hbm),
         scratch_shapes=[
             pltpu.VMEM(slab.shape, jnp.float32),
+            pltpu.VMEM((4 * width, count * wide), jnp.bfloat16),
             pltpu.VMEM((3 * width, count * wide), jnp.bfloat16),
             pltpu.VMEM(outputs[1].shape, jnp.float32),
             pltpu.VMEM(outputs[2].shape, jnp.float32),
@@ -198,7 +202,7 @@
     arrived = lax.ppermute(lead, "row", [(0, 1)])
     leads = [jnp.where(row_index == 1, arrived, lead)]
     which = jnp.zeros_like(row_index)
-    for i in (4, 2, 6):
+    for i in (6, 4, 2):
         which = jnp.where(row_index // 2 * 2 == i, len(leads), which)
         leads.append(lax.ppermute(leads[0], "row", [(0, i), (1, i + 1)]))
     place = jnp.stack([(row_index == 0).astype(jnp.int32), which, lax.axis_index("col")])

time: 45.6 us -> 45.6 us (level)
    ppermute x3, waiting for transfers between devices: 5.08 us -> 7.24 us  [body(): leads.append(lax.ppermute(leads[0], 'row', [(0, i), (1, i + 1)]))]
    all_to_all x1, waiting for transfers between devices: 3.56 us -> 1.41 us  [body(): two = lax.all_to_all(second, 'col', split_axis=0, concat_axis=0)]
where the time goes in v7:
time: 45.6 us; the launch traced here: 45 us
  waiting for transfers between devices  19 us (42%)
  starting transfers between devices  14.8 us (32%)
  Pallas kernels  9.59 us (21%)
  local copies, waits for them, and re-layouts  0.78 us (2%)
  between operations  0.74 us (2%)
    all_to_all x1, waiting for transfers between devices, body(): one = lax.all_to_all(first, 'col', split_axis=0, concat_axis=0)  10.3 us
    all_to_all x1, starting transfers between devices, body(): one = lax.all_to_all(first, 'col', split_axis=0, concat_axis=0)  7.88 us
    ppermute x3, waiting for transfers between devices, body(): leads.append(lax.ppermute(leads[0], 'row', [(0, i), (1, i + 1)]))  7.24 us
    pallas_call x1, Pallas kernels, step(): pl.pallas_call(step_kernel, out_shape=outputs, in_specs=[pl.BlockSpec(mem...  5.98 us
    pallas_call x2, Pallas kernels, pack(): pl.pallas_call(pack_kernel, grid=(1,), out_shape=jax.ShapeDtypeStruct(sen...  3.61 us
    all_to_all x1, starting transfers between devices, body(): two = lax.all_to_all(second, 'col', split_axis=0, concat_axis=0)  3.59 us
    ppermute x3, starting transfers between devices, body(): leads.append(lax.ppermute(leads[0], 'row', [(0, i), (1, i + 1)]))  2.63 us
    all_to_all x1, waiting for transfers between devices, body(): two = lax.all_to_all(second, 'col', split_axis=0, concat_axis=0)  1.41 us
  transfers between devices with their start and end apart: 6, of which 3 were waited for; matrix products, arithmetic and copies ran while one was open for 2% of the time, Pallas kernels for 4%

profile of v7, /device:TPU:24, one launch (start us, length us, event | category | flops | bytes accessed | tf_op | source)
XLA Modules:
  0.0 45.0 jit_solution(17107788928801924752)
XLA Ops:
  0.6 1.8 %pack_pieces.2 = f32[16,80,128]{2,1,0:T(8,128)} custom-call(f32[64,256]{1,0:T(8,128)} %panel_ref.2, f32[16,16,256]{2,1,0:T(8,128)} %bitcast.6), custom_call_target="tpu_custom_call" | custom-call | tf_op jit(solution)/shard_map/pack_pieces/pallas_call | solution.py:76
  2.4 7.9 %all-to-all-start = ((f32[16,80,128]{2,1,0:T(8,128)}), f32[16,80,128]{2,1,0:T(8,128)S(1)}, u32[]{:S(2)}, u32[]{:S(2)}) async-start(f32[16,80,128]{2,1,0:T(8,128)} %pack_pieces.2), calls=%async_computation | async-start | bytes 1310720 | tf_op jit(solution)/shard_map/all_to_all | solution.py:197
  10.3 1.8 %pack_pieces.3 = f32[16,80,128]{2,1,0:T(8,128)} custom-call(f32[64,256]{1,0:T(8,128)} %panel_ref.2, f32[16,16,256]{2,1,0:T(8,128)} %bitcast.7), custom_call_target="tpu_custom_call" | custom-call | tf_op jit(solution)/shard_map/pack_pieces/pallas_call | solution.py:76
  12.1 0.8 %fusion = (f32[64,128]{1,0:T(8,128)S(1)}, f32[64,128]{1,0:T(8,128)S(1)}) fusion(f32[4096,256]{1,0:T(8,128)} %slab_ref.1), kind=kLoop, calls=%fused_computation.5 | loop fusion | bytes 131072 | tf_op jit(solution)/shard_map/slice | solution.py:198
  12.9 10.3 %all-to-all-done.one_ref = f32[16,80,128]{2,1,0:T(8,128)S(1)} async-done(((f32[16,80,128]{2,1,0:T(8,128)}), f32[16,80,128]{2,1,0:T(8,128)S(1)}, u32[]{:S(2)}, u32[]{:S(2)}) %all-to-all-start) | async-done | bytes 655392 | tf_op jit(solution)/shard_map/all_to_all | solution.py:197
  23.3 3.6 %all-to-all-start.1 = ((f32[16,80,128]{2,1,0:T(8,128)}), f32[16,80,128]{2,1,0:T(8,128)S(1)}, u32[]{:S(2)}, u32[]{:S(2)}) async-start(f32[16,80,128]{2,1,0:T(8,128)} %pack_pieces.3), calls=%async_computation.1 | async-start | bytes 1310720 | tf_op jit(solution)/shard_map/all_to_all | solution.py:200
  26.9 0.7 %collective-permute-start = (f32[208,128]{1,0:T(8,128)S(1)}, f32[208,128]{1,0:T(8,128)S(1)}, u32[]{:S(2)}, u32[]{:S(2)}) collective-permute-start(f32[208,128]{1,0:T(8,128)S(1)} %pad_maximum_fusion), channel_id=1, source_target_pairs={{0,16},{1,17},{2,18},{3,19},{4,20},{5,21},{6,22},{7,23},{8,24},{9,... | collective-permute-start | bytes 319496 | tf_op jit(solution)/shard_map/ppermute | solution.py:202
  27.6 0.0 collective-permute-done
  27.6 0.7 %collective-permute-start.3 = (f32[208,128]{1,0:T(8,128)S(1)}, f32[208,128]{1,0:T(8,128)S(1)}, u32[]{:S(2)}, u32[]{:S(2)}) collective-permute-start(f32[208,128]{1,0:T(8,128)S(1)} %broadcast_select_fusion.lead0_ref), channel_id=1, source_target_pairs={{0,32},{16,48},{1,33},{17,49},{2,34},{18,50},{3,35},{19,51},{4,36}... | collective-permute-start | bytes 319496 | tf_op jit(solution)/shard_map/ppermute | solution.py:207
  28.3 0.7 %collective-permute-start.2 = (f32[208,128]{1,0:T(8,128)S(1)}, f32[208,128]{1,0:T(8,128)S(1)}, u32[]{:S(2)}, u32[]{:S(2)}) collective-permute-start(f32[208,128]{1,0:T(8,128)S(1)} %broadcast_select_fusion.lead0_ref), channel_id=1, source_target_pairs={{0,64},{16,80},{1,65},{17,81},{2,66},{18,82},{3,67},{19,83},{4,68}... | collective-permute-start | bytes 319496 | tf_op jit(solution)/shard_map/ppermute | solution.py:207
  29.0 1.3 %collective-permute-start.1 = (f32[208,128]{1,0:T(8,128)S(1)}, f32[208,128]{1,0:T(8,128)S(1)}, u32[]{:S(2)}, u32[]{:S(2)}) collective-permute-start(f32[208,128]{1,0:T(8,128)S(1)} %broadcast_select_fusion.lead0_ref), channel_id=1, source_target_pairs={{0,96},{16,112},{1,97},{17,113},{2,98},{18,114},{3,99},{19,115},{4... | collective-permute-start | bytes 319496 | tf_op jit(solution)/shard_map/ppermute | solution.py:207
  30.3 0.1 pad_add_fusion.place_ref
  30.4 0.0 collective-permute-done.3.lead3_ref
  30.4 0.0 collective-permute-done.2.lead2_ref
  30.4 7.2 %collective-permute-done.1.lead1_ref = f32[208,128]{1,0:T(8,128)S(1)} collective-permute-done((f32[208,128]{1,0:T(8,128)S(1)}, f32[208,128]{1,0:T(8,128)S(1)}, u32[]{:S(2)}, u32[]{:S(2)}) %collective-permute-start.1) | collective-permute-done | bytes 106528 | tf_op jit(solution)/shard_map/ppermute | solution.py:207
  37.6 1.4 %all-to-all-done.1.two_ref = f32[16,80,128]{2,1,0:T(8,128)S(1)} async-done(((f32[16,80,128]{2,1,0:T(8,128)}), f32[16,80,128]{2,1,0:T(8,128)S(1)}, u32[]{:S(2)}, u32[]{:S(2)}) %all-to-all-start.1) | async-done | bytes 655392 | tf_op jit(solution)/shard_map/all_to_all | solution.py:200
  39.0 6.0 %factor_and_update.1 = (f32[4096,256]{1,0:T(8,128)}, f32[16,4096]{1,0:T(8,128)}, f32[64,256]{1,0:T(8,128)}) custom-call(s32[3]{0:T(128)S(1)} %pad_add_fusion.place_ref, f32[16,80,128]{2,1,0:T(8,128)S(1)} %all-to-all-done.one_ref, f32[16,80,128]{2,1,0:T(8,128)S(1)} %all-to-all-done.1.two_ref, f32[208,128]{1,0:T(8,128)S(1)} %broadcast_select_fusion.lead0_ref, ...), custom_call_target="tpu_custom_call" | custom-call | flops 402653184 | bytes 8388608 | tf_op jit(solution)/shard_map/factor_and_update/pallas_call | solution.py:164
  (4 shorter events, 0.0 us)
Async XLA Ops:
  2.4 20.8 %all-to-all-start = ((f32[16,80,128]{2,1,0:T(8,128)}), f32[16,80,128]{2,1,0:T(8,128)S(1)}, u32[]{:S(2)}, u32[]{:S(2)}) async-start(f32[16,80,128]{2,1,0:T(8,128)} %pack_pieces.2), calls=%async_computation | async-start | bytes 1310720 | tf_op jit(solution)/shard_map/all_to_all | solution.py:197
  23.3 15.7 %all-to-all-start.1 = ((f32[16,80,128]{2,1,0:T(8,128)}), f32[16,80,128]{2,1,0:T(8,128)S(1)}, u32[]{:S(2)}, u32[]{:S(2)}) async-start(f32[16,80,128]{2,1,0:T(8,128)} %pack_pieces.3), calls=%async_computation.1 | async-start | bytes 1310720 | tf_op jit(solution)/shard_map/all_to_all | solution.py:200
  26.9 0.7 %collective-permute-start = (f32[208,128]{1,0:T(8,128)S(1)}, f32[208,128]{1,0:T(8,128)S(1)}, u32[]{:S(2)}, u32[]{:S(2)}) collective-permute-start(f32[208,128]{1,0:T(8,128)S(1)} %pad_maximum_fusion), channel_id=1, source_target_pairs={{0,16},{1,17},{2,18},{3,19},{4,20},{5,21},{6,22},{7,23},{8,24},{9,... | collective-permute-start | bytes 319496 | tf_op jit(solution)/shard_map/ppermute | solution.py:202
  27.6 2.7 %collective-permute-start.3 = (f32[208,128]{1,0:T(8,128)S(1)}, f32[208,128]{1,0:T(8,128)S(1)}, u32[]{:S(2)}, u32[]{:S(2)}) collective-permute-start(f32[208,128]{1,0:T(8,128)S(1)} %broadcast_select_fusion.lead0_ref), channel_id=1, source_target_pairs={{0,32},{16,48},{1,33},{17,49},{2,34},{18,50},{3,35},{19,51},{4,36}... | collective-permute-start | bytes 319496 | tf_op jit(solution)/shard_map/ppermute | solution.py:207
  28.3 2.1 %collective-permute-start.2 = (f32[208,128]{1,0:T(8,128)S(1)}, f32[208,128]{1,0:T(8,128)S(1)}, u32[]{:S(2)}, u32[]{:S(2)}) collective-permute-start(f32[208,128]{1,0:T(8,128)S(1)} %broadcast_select_fusion.lead0_ref), channel_id=1, source_target_pairs={{0,64},{16,80},{1,65},{17,81},{2,66},{18,82},{3,67},{19,83},{4,68}... | collective-permute-start | bytes 319496 | tf_op jit(solution)/shard_map/ppermute | solution.py:207
  29.0 8.6 %collective-permute-start.1 = (f32[208,128]{1,0:T(8,128)S(1)}, f32[208,128]{1,0:T(8,128)S(1)}, u32[]{:S(2)}, u32[]{:S(2)}) collective-permute-start(f32[208,128]{1,0:T(8,128)S(1)} %broadcast_select_fusion.lead0_ref), channel_id=1, source_target_pairs={{0,96},{16,112},{1,97},{17,113},{2,98},{18,114},{3,99},{19,115},{4... | collective-permute-start | bytes 319496 | tf_op jit(solution)/shard_map/ppermute | solution.py:207
